TPU v7x, 512 devices: a whole 4x4x16 slice. The times are simulated.
512 devices in a mesh: sample: 8 (over x, z_hi), ctx: 64 (over z_lo, y, core).
Axes of the slice: x: 4, y: 4, z: 16 (z_hi: 2, z_lo: 8; z = z_hi * 8 + z_lo), core: 2. Of those that a mesh axis runs over, the one named last changes fastest.
Arguments:
- queries: bfloat16 [16, 512, 8192], P('sample', None, 'ctx'), may hold values from -8 to 8
- prompt_key_value: bfloat16 [2, 2048, 1024], P(None, 'ctx', 'sample'), may hold values from -6 to 6
- continuation_key_value: bfloat16 [2, 16, 512, 1024], P(None, 'sample', 'ctx'), may hold values from -6 to 6
- page_owner: int32 [2048], replicated, may hold values from 0 to 16, as said below
- cont_lengths: int32 [16], replicated, may hold values from 2 to 512, as said below
- branch_offsets: int32 [16], replicated, may hold values from 512 to 2048
Outputs:
- attended: bfloat16 [16, 512, 8192], P('sample', None, 'ctx')
Inputs may be any that keep to these rules, and one draw needn't show every extreme that they name: `page_owner`: constant over each aligned page of 16 positions; 0 marks a page seen by every continuation that branches after it, s + 1 a page seen only by continuation s; some page belongs to continuation 16 - 1. `cont_lengths`: some continuation has all 512 positions live.
All inputs are finite; a program needn't handle non-finite values.
Results may differ from a plain program's by a relative error of at most 0.0045.
Values may be sent and summed in bfloat16 or wider, within the bound.
No kernel may reach another device: no remote copies, remote signals or barrier semaphores. Data moves between devices by JAX's collectives and lax.ppermute only.
A program may use at most 64 MiB of HBM per device.

v0:
```python
import jax
import jax.numpy as jnp
from jax import lax
from jax.sharding import PartitionSpec as P

QUERY_HEADS = 64
KEY_VALUE_HEADS = 8
HEAD_SIZE = 128


neg_large = -1e30
key_block = 256


def attend_part(running, grouped, keys_part, values_part, visible):
    largest, weight_sum, summed = running
    scale = grouped.shape[-1] ** (-0.5)
    if keys_part.ndim == 2:
        scores = jnp.einsum("sthd,nd->sthn", grouped, keys_part, preferred_element_type=jnp.float32)
    else:
        scores = jnp.einsum(
            "sthd,snd->sthn", grouped, keys_part, preferred_element_type=jnp.float32
        )
    cover = visible[:, :, None, :]
    scores = jnp.where(cover, scores * scale, neg_large)
    new_max = jnp.maximum(largest, jnp.max(scores, axis=-1))
    weights = jnp.where(cover, jnp.exp(scores - new_max[..., None]), 0.0)
    rescale = jnp.exp(largest - new_max)
    weight_sum = weight_sum * rescale + jnp.sum(weights, axis=-1)
    rounded = weights.astype(jnp.bfloat16)
    if values_part.ndim == 2:
        product = jnp.einsum(
            "sthn,nd->sthd", rounded, values_part, preferred_element_type=jnp.float32
        )
    else:
        product = jnp.einsum(
            "sthn,snd->sthd", rounded, values_part, preferred_element_type=jnp.float32
        )
    summed = summed * rescale[..., None] + product
    return (new_max, weight_sum, summed)


def attend_blocks(running, grouped, keys_all, values_all, visible, key_axis):
    count_keys = keys_all.shape[key_axis]
    for block_begin in range(0, count_keys, key_block):
        block_end = min(block_begin + key_block, count_keys)
        keys_part = lax.slice_in_dim(keys_all, block_begin, block_end, axis=key_axis)
        values_part = lax.slice_in_dim(values_all, block_begin, block_end, axis=key_axis)
        running = attend_part(
            running, grouped, keys_part, values_part, visible[:, :, block_begin:block_end]
        )
    return running


def initial_state(grouped):
    largest = jnp.full(grouped.shape[:3], neg_large, jnp.float32)
    weight_sum = jnp.zeros(grouped.shape[:3], jnp.float32)
    summed = jnp.zeros(grouped.shape, jnp.float32)
    return (largest, weight_sum, summed)


def prompt_step(grouped, page_owner, offsets_here, sample_ids, column_start):

    def fold_prompt(running, portion, first_row):
        count_keys = portion.shape[1]
        picked = lax.dynamic_slice_in_dim(portion, column_start, HEAD_SIZE, 2)
        positions = jnp.arange(count_keys, dtype=jnp.int32)
        allowed = (page_owner[None, :] == 0) | (page_owner[None, :] == sample_ids[:, None] + 1)
        seen = allowed & (positions[None, :] < offsets_here[:, None])
        return attend_blocks(running, grouped, picked[0], picked[1], seen[:, None, :], 0)

    return fold_prompt


def local(
    queries, prompt_key_value, continuation_key_value, page_owner, cont_lengths, branch_offsets
):
    sequence_local, cont_len, width = queries.shape
    heads_here = width // HEAD_SIZE
    query_groups = QUERY_HEADS // KEY_VALUE_HEADS
    context_count = lax.axis_size("ctx")
    copy_count = context_count // KEY_VALUE_HEADS
    kv_head = lax.axis_index("ctx") * heads_here // query_groups
    base_sample = lax.axis_index("sample") * sequence_local
    sample_ids = base_sample + jnp.arange(sequence_local, dtype=jnp.int32)
    offsets_here = lax.dynamic_slice_in_dim(branch_offsets, base_sample, sequence_local)
    lengths_here = lax.dynamic_slice_in_dim(cont_lengths, base_sample, sequence_local)
    query_pos = jnp.arange(cont_len, dtype=jnp.int32)
    grouped = queries.reshape(sequence_local, cont_len, heads_here, HEAD_SIZE)
    full_heads = lax.all_gather(prompt_key_value, "sample", axis=2, tiled=True)
    fold_prompt = prompt_step(grouped, page_owner, offsets_here, sample_ids, kv_head * HEAD_SIZE)
    running = fold_prompt(
        initial_state(grouped), lax.all_gather(full_heads, "ctx", axis=1, tiled=True), jnp.int32(0)
    )
    continuation_block = continuation_key_value.shape[2]
    spread_continuation = jnp.repeat(
        continuation_key_value.reshape(
            2, sequence_local, continuation_block, KEY_VALUE_HEADS, HEAD_SIZE
        ),
        copy_count,
        axis=3,
    )
    own_cont = lax.all_to_all(spread_continuation, "ctx", split_axis=3, concat_axis=2, tiled=True)
    own_cont = own_cont.reshape(2, sequence_local, continuation_block * context_count, HEAD_SIZE)
    causal = query_pos[None, :, None] >= query_pos[None, None, :]
    live_keys = query_pos[None, None, :] < lengths_here[:, None, None]
    visible = causal & live_keys
    running = attend_blocks(running, grouped, own_cont[0], own_cont[1], visible, 1)
    largest, weight_sum, summed = running
    mixed = summed / weight_sum[..., None]
    live_rows = (query_pos[None, :] < lengths_here[:, None])[:, :, None, None]
    mixed = jnp.where(live_rows, mixed, 0.0)
    return mixed.reshape(sequence_local, cont_len, width).astype(jnp.bfloat16)


def solution(mesh):
    in_specs = (
        P("sample", None, "ctx"),
        P(None, "ctx", "sample"),
        P(None, "sample", "ctx", None),
        P(),
        P(),
        P(),
    )
    out_specs = P("sample", None, "ctx")
    return jax.shard_map(local, mesh=mesh, in_specs=in_specs, out_specs=out_specs, check_vma=False)
```

profile of v0, /device:TPU:1, one launch (start us, length us, event | category | flops | bytes accessed | tf_op | source)
XLA Modules:
  0.0 243.9 jit_solution(1014503203489306723)
XLA Ops:
  6.5 0.0 copy-start
  6.5 0.0 all-gather.2.cloned.1.call-start
  6.5 61.0 %all_gather.6 = bf16[2,32,1024]{2,1,0:T(8,128)(2,1)} all-gather(bf16[2,32,128]{2,1,0:T(8,128)(2,1)} %param.7), channel_id=1, replica_groups=mesh['sample'=8,'ctx'=64] {'sample'}, dimensions={2}, use_global_device_ids=true | all-gather | bytes 147456 | tf_op jit(solution)/shard_map/all_gather | solution.py:90
  67.5 0.0 all-gather.2.cloned.1.call-update
  67.5 0.9 copy.25
  68.4 0.9 broadcast_in_dim.196
  69.3 18.3 %all-to-all-start = ((bf16[2,2,8,64,128]{4,2,1,0,3:T(8,128)(2,1)}), bf16[2,2,8,64,128]{4,2,1,0,3:T(8,128)(2,1)S(1)}, u32[]{:S(2)}, u32[]{:S(2)}) async-start(bf16[2,2,8,64,128]{4,2,1,0,3:T(8,128)(2,1)} %bitcast.49), calls=%async_computation | async-start | bytes 1048576 | tf_op jit(solution)/shard_map/all_to_all | solution.py:103
  87.6 0.7 dynamic_slice.9
  88.3 0.7 dynamic_slice.10
  89.1 0.1 iota_compare_fusion
  89.2 0.1 iota_compare_fusion.1
  89.2 0.7 broadcast_compare_fusion
  89.9 0.8 compare_and_fusion
  90.7 0.3 broadcast_and_fusion
  91.1 31.7 %all-to-all-done = bf16[2,2,8,64,128]{4,2,1,0,3:T(8,128)(2,1)S(1)} async-done(((bf16[2,2,8,64,128]{4,2,1,0,3:T(8,128)(2,1)}), bf16[2,2,8,64,128]{4,2,1,0,3:T(8,128)(2,1)S(1)}, u32[]{:S(2)}, u32[]{:S(2)}) %all-to-all-start) | async-done | bytes 524320 | tf_op jit(solution)/shard_map/all_to_all | solution.py:103
  122.8 0.0 copy-done
  122.8 0.4 fusion.119
  123.2 0.4 fusion.120
  123.7 88.4 %all-gather.2.cloned.1.call-done = bf16[2,2048,1024]{2,1,0:T(8,128)(2,1)} async-done(((bf16[2,32,1024]{2,1,0:T(8,128)(2,1)}), bf16[2,2048,1024]{2,1,0:T(8,128)(2,1)}) %all-gather.2.cloned.1.call-update) | async-done | bytes 8388624 | tf_op jit(solution)/shard_map/all_gather | solution.py:93
  212.1 1.2 fusion.128
  213.2 1.2 fusion.121
  214.4 1.2 fusion.122
  215.6 1.2 fusion.123
  216.8 1.2 fusion.124
  217.9 1.2 fusion.125
  219.1 1.2 fusion.126
  220.3 1.2 fusion.127
  221.5 0.5 fusion.52
  222.0 0.7 fusion.48
  222.7 0.5 fusion.54
  223.2 0.5 fusion.32
  223.7 0.4 fusion.44
  224.1 0.4 fusion.40
  224.5 0.4 fusion.36
  225.0 0.1 multiply_add_fusion
  225.1 1.5 fusion.27
  226.5 1.3 fusion.26
  227.9 1.3 fusion.25
  229.2 1.3 fusion.24
  230.5 1.3 fusion.23
  231.8 1.3 fusion.22
  233.2 1.3 fusion.21
  234.5 2.6 %fusion.31 = bf16[2,512,128]{2,1,0:T(8,128)(2,1)} fusion(f32[2,512,128]{2,1,0:T(8,128)S(1)} %fusion.52, f32[2,512,128]{2,1,0:T(8,128)S(1)} %fusion.54, f32[2,512,128]{2,1,0:T(8,128)S(1)} %fusion.21, f32[2,512,256]{1,2,0:T(8,128)S(1)} %get-tuple-element.43, f32[2,512]{1,0:T(2,128)S(1)} %get-tuple-element.19, pred[2,256]{1,0:T(4,128)(4,1)S(1)} %get-tuple-element.29, ...), kind=kOutput, calls=%fused_computation.49 | convolution fusion | flops 68943872 | bytes 2967052 | tf_op jit(solution)/shard_map/sthn,nd->sthd/dot_general | solution.py:32
  (6 shorter events, 0.1 us)
Async XLA Ops:
  6.5 116.3 %copy-start = (bf16[2,512,128]{2,1,0:T(8,128)(2,1)S(1)}, bf16[2,512,128]{2,1,0:T(8,128)(2,1)}, u32[]{:S(2)}) copy-start(bf16[2,512,128]{2,1,0:T(8,128)(2,1)} %param.6) | copy-start | bytes 786436
  6.5 205.5 %all-gather.2.cloned.1.call-start = ((), (), s32[]{:S(2)}) async-start(), calls=%async_computation.1 | async-start | bytes 8519680 | tf_op jit(solution)/shard_map/all_gather | solution.py:93
  69.3 53.4 %all-to-all-start = ((bf16[2,2,8,64,128]{4,2,1,0,3:T(8,128)(2,1)}), bf16[2,2,8,64,128]{4,2,1,0,3:T(8,128)(2,1)S(1)}, u32[]{:S(2)}, u32[]{:S(2)}) async-start(bf16[2,2,8,64,128]{4,2,1,0,3:T(8,128)(2,1)} %bitcast.49), calls=%async_computation | async-start | bytes 1048576 | tf_op jit(solution)/shard_map/all_to_all | solution.py:103
Sparse Core Ops, SparseCore 0:
  67.7 144.3 all-gather.1
where the time goes:
time: 245 us; the launch traced here: 244 us
  waiting for transfers between devices  120 us (49%)
  blocking collectives  61 us (25%)
  matrix products  23.1 us (9%)
  starting transfers between devices  18.3 us (7%)
  between operations  13.6 us (6%)
  other arithmetic  4.54 us (2%)
  local copies, waits for them, and re-layouts  3.33 us (1%)
    all_gather x1, waiting for transfers between devices, local(): lax.all_gather(full_heads, 'ctx', axis=1, tiled=True)  88.4 us
    all_gather x1, blocking collectives, local(): full_heads = lax.all_gather(prompt_key_value, 'sample', axis=2, tiled=True)  61 us
    all_to_all x1, waiting for transfers between devices, local(): lax.all_to_all(spread_continuation, 'ctx', split_axis=3, concat_axis=2, t...  31.7 us
    all_to_all x1, starting transfers between devices, local(): lax.all_to_all(spread_continuation, 'ctx', split_axis=3, concat_axis=2, t...  18.3 us
    dot_general x8, matrix products, attend_part(): jnp.einsum('sthn,nd->sthd', rounded, values_part, preferred_element_type=...  11.9 us
    dot_general x8, matrix products, attend_part(): jnp.einsum('sthd,nd->sthn', grouped, keys_part, preferred_element_type=jn...  9.32 us
  transfers between devices with their start and end apart: 2, of which 2 were waited for; matrix products, arithmetic and copies ran while one was open for 3% of the time, Pallas kernels for 0%

commit v1 on v0

v1 whole, which is shorter than its diff:
```python
import jax
import jax.numpy as jnp
from jax import lax
from jax.experimental import pallas as pl
from jax.experimental.pallas import tpu as pltpu
from jax.sharding import Mesh, PartitionSpec as P

HEAD_SIZE = 128
KEY_VALUE_HEADS = 8
AXES = ("x", "zh", "zl", "y", "c")
DIMS = (4, 2, 8, 4, 2)
NEG = -1e30
LOG2E = 1.4426950408889634
ROWS = 256


def flat(x, zh, zl, y, c):
    return (((x * 2 + zh) * 8 + zl) * 4 + y) * 2 + c


def block_moves(flip):
    moves = []
    for s in range(8):
        for a in range(8):
            for y in range(4):
                for c in range(2):
                    source = flat(s // 2, s % 2, a, y, c)
                    moves.append((source, flat(a // 2, (a % 2) ^ flip, s, y, c)))
    return moves


def attend(q_ref, own_ref, other_ref, cont_ref, owner_ref, lengths_ref, offsets_ref, out_ref):
    tile = pl.program_id(0)
    per_sample = 512 // ROWS
    here = tile // per_sample
    row0 = (tile % per_sample) * ROWS
    core = lax.axis_index("c")
    flip = lax.axis_index("zh")
    sample = (lax.axis_index("x") * 2 + lax.axis_index("zh")) * 2 + here
    length = lengths_ref[sample]
    offset = offsets_ref[sample]
    q = q_ref[0]
    dims = (((1,), (1,)), ((), ()))
    col = lax.broadcasted_iota(jnp.int32, (1, 1024), 1)
    block = ((col >> 5) & 1) ^ flip
    base = ((2 * (col >> 8) + block) * 4 + ((col >> 6) & 3)) * 64 + (col & 31)
    scores = []
    for ref, which in ((own_ref, core), (other_ref, 1 - core)):
        owner = owner_ref[flip, which].reshape(1, 1024)
        place = base + which * 32
        seen = ((owner == 0) | (owner == sample + 1)) & (place < offset)
        bias = jnp.where(seen, 0.0, NEG)
        keys = ref[:, :, 0].reshape(1024, HEAD_SIZE)
        part = lax.dot_general(q, keys, dims, preferred_element_type=jnp.float32)
        scores.append(part + bias)
    ucol = lax.broadcasted_iota(jnp.int32, (1, 512), 1)
    swap = (ucol >> 8) ^ core
    u = (((ucol >> 3) & 7) * 8 + ((ucol >> 6) & 3) * 2 + swap) * 8 + (ucol & 7)
    t = row0 + lax.broadcasted_iota(jnp.int32, (ROWS, 1), 0)
    part = lax.dot_general(q, cont_ref[0, 0], dims, preferred_element_type=jnp.float32)
    scores.append(jnp.where((u <= t) & (u < length), part, NEG))
    top = scores[0].max(axis=1, keepdims=True)
    for part in scores[1:]:
        top = jnp.maximum(top, part.max(axis=1, keepdims=True))
    total = jnp.zeros((ROWS, 1), jnp.float32)
    mixed = jnp.zeros((ROWS, HEAD_SIZE), jnp.float32)
    values = (
        own_ref[:, :, 1].reshape(1024, HEAD_SIZE),
        other_ref[:, :, 1].reshape(1024, HEAD_SIZE),
        cont_ref[1, 0],
    )
    for part, value in zip(scores, values):
        weights = jnp.exp2((part - top) * (HEAD_SIZE**-0.5 * LOG2E))
        total += weights.sum(axis=1, keepdims=True)
        mixed += jnp.dot(weights.astype(jnp.bfloat16), value, preferred_element_type=jnp.float32)
    out_ref[0] = jnp.where(t < length, mixed / total, 0.0).astype(jnp.bfloat16)


def local(queries, prompt, cont, page_owner, cont_lengths, branch_offsets):
    first = lax.ppermute(prompt, AXES, block_moves(0))
    second = lax.ppermute(prompt, AXES, block_moves(1))
    pieces = cont.reshape(2, 2, 8, KEY_VALUE_HEADS, HEAD_SIZE).transpose(3, 0, 1, 2, 4)
    pieces = lax.all_to_all(pieces, "zl", 0, 0, tiled=True)
    pair = jnp.stack([first, second])
    spread = jnp.broadcast_to(pair[None], (16,) + pair.shape)
    own = lax.all_to_all(spread, ("x", "y"), 0, 0, tiled=True)
    spread = jnp.broadcast_to(pieces[None], (4,) + pieces.shape)
    pieces = lax.all_to_all(spread, "y", 0, 0, tiled=True)
    pieces = pieces.transpose(2, 3, 0, 1, 4, 5).reshape(2, 2, 256, HEAD_SIZE)
    swap = [(0, 1), (1, 0)]
    other = lax.ppermute(own, "c", swap)
    far = lax.ppermute(pieces, "c", swap)
    own_cont = jnp.concatenate([pieces, far], axis=2)
    owner = page_owner.reshape(4, 2, 4, 2, 32).transpose(3, 0, 2, 1, 4)
    owner = jnp.stack([owner, owner[:, :, :, ::-1]]).reshape(2, 2, 8, 128)
    per_sample = 512 // ROWS
    return pl.pallas_call(
        attend,
        grid=(2 * per_sample,),
        out_shape=jax.ShapeDtypeStruct(queries.shape, jnp.bfloat16),
        in_specs=[
            pl.BlockSpec((1, ROWS, HEAD_SIZE), lambda i: (i // per_sample, i % per_sample, 0)),
            pl.BlockSpec((16, 2, 2, 32, HEAD_SIZE), lambda i: (0, 0, 0, 0, 0)),
            pl.BlockSpec((16, 2, 2, 32, HEAD_SIZE), lambda i: (0, 0, 0, 0, 0)),
            pl.BlockSpec((2, 1, 512, HEAD_SIZE), lambda i: (0, i // per_sample, 0, 0)),
            pl.BlockSpec((2, 2, 8, 128), lambda i: (0, 0, 0, 0)),
            pl.BlockSpec(memory_space=pltpu.SMEM),
            pl.BlockSpec(memory_space=pltpu.SMEM),
        ],
        out_specs=pl.BlockSpec(
            (1, ROWS, HEAD_SIZE), lambda i: (i // per_sample, i % per_sample, 0)
        ),
        cost_estimate=pl.CostEstimate(
            flops=1400000000, transcendentals=2700000, bytes_accessed=3000000
        ),
    )(queries, own, other, own_cont, owner, cont_lengths, branch_offsets)


def solution(mesh):
    fine = Mesh(mesh.devices.reshape(DIMS), AXES)
    sample, ctx = ("x", "zh"), ("zl", "y", "c")
    in_specs = (
        P(sample, None, ctx),
        P(None, ctx, sample),
        P(None, sample, ctx, None),
        P(),
        P(),
        P(),
    )
    return jax.shard_map(
        local, mesh=fine, in_specs=in_specs, out_specs=P(sample, None, ctx), check_vma=False
    )
```

time: 245 us -> 79.2 us (0.32)
  waiting for transfers between devices: 120 us -> 10.2 us
  blocking collectives: 61 us -> 0 us
  starting transfers between devices: 18.3 us -> 55 us
  matrix products: 23.1 us -> 0 us
  between operations: 13.6 us -> 0.14 us
  Pallas kernels: 0 us -> 7.4 us
  other arithmetic: 4.54 us -> 1.48 us
    all_gather x1 -> x0, waiting for transfers between devices: 88.4 us -> none  [local(): lax.all_gather(full_heads, 'ctx', axis=1, tiled=True)]
    all_gather x1 -> x0, blocking collectives: 61 us -> none  [local(): full_heads = lax.all_gather(prompt_key_value, 'sample', axis=2, tiled=True)]
    dot_general x20 -> x0, matrix products: 23.1 us -> none  [the longest x8 11.9 us: attend_part(): jnp.einsum('sthn,nd->sthd', rounded, values_part, preferred_element_type=...]
    all_to_all x1 -> x3, waiting for transfers between devices: 31.7 us -> 9.87 us  [the longest x1 8.93 us: local(): own = lax.all_to_all(spread, ('x', 'y'), 0, 0, tiled=True)]
    ppermute x0 -> x4, starting transfers between devices: none -> 21.2 us  [the longest x1 7.94 us: local(): second = lax.ppermute(prompt, AXES, block_moves(1))]
    all_to_all x1 -> x3, starting transfers between devices: 18.3 us -> 33.8 us  [the longest x1 17.2 us: local(): own = lax.all_to_all(spread, ('x', 'y'), 0, 0, tiled=True)]
    pallas_call x0 -> x1, Pallas kernels: none -> 7.4 us  [local(): pl.pallas_call(attend, grid=(2 * per_sample,), out_shape=jax.ShapeDtypeSt...]
    reduce_sum x5 -> x0, other arithmetic: 2.48 us -> none  [attend_part(): weight_sum = weight_sum * rescale + jnp.sum(weights, axis=-1)]
  transfers between devices with their start and end apart: 2 -> 7, of which waited for: 2 -> 4; matrix products, arithmetic and copies ran while one was open for 3% -> 2% of each run, Pallas kernels for 0% -> 0%
where the time goes in v1:
time: 79.2 us; the launch traced here: 78.6 us
  starting transfers between devices  55 us (69%)
  waiting for transfers between devices  10.2 us (13%)
  Pallas kernels  7.4 us (9%)
  local copies, waits for them, and re-layouts  4.37 us (6%)
  other arithmetic  1.48 us (2%)
    all_to_all x1, starting transfers between devices, local(): own = lax.all_to_all(spread, ('x', 'y'), 0, 0, tiled=True)  17.2 us
    all_to_all x1, starting transfers between devices, local(): pieces = lax.all_to_all(pieces, 'zl', 0, 0, tiled=True)  13.2 us
    all_to_all x1, waiting for transfers between devices, local(): own = lax.all_to_all(spread, ('x', 'y'), 0, 0, tiled=True)  8.93 us
    ppermute x1, starting transfers between devices, local(): second = lax.ppermute(prompt, AXES, block_moves(1))  7.94 us
    pallas_call x1, Pallas kernels, local(): pl.pallas_call(attend, grid=(2 * per_sample,), out_shape=jax.ShapeDtypeSt...  7.4 us
    ppermute x1, starting transfers between devices, local(): far = lax.ppermute(pieces, 'c', swap)  6.61 us
    ppermute x1, starting transfers between devices, local(): other = lax.ppermute(own, 'c', swap)  6 us
    all_to_all x1, starting transfers between devices, local(): pieces = lax.all_to_all(spread, 'y', 0, 0, tiled=True)  3.41 us
  transfers between devices with their start and end apart: 7, of which 4 were waited for; matrix products, arithmetic and copies ran while one was open for 2% of the time, Pallas kernels for 0%

profile of v1, /device:TPU:1, one launch (start us, length us, event | category | flops | bytes accessed | tf_op | source)
XLA Modules:
  0.0 78.6 jit_solution(8672684229051839869)
XLA Ops:
  0.0 1.5 %copy.13 = bf16[8,2,2,8,128]{4,3,2,1,0:T(8,128)(2,1)} copy(bf16[8,2,2,8,128]{4,3,0,2,1:T(8,128)(2,1)} %bitcast.19) | data formatting | bytes 131072 | tf_op jit(solution)/shard_map/transpose | solution.py:82
  1.5 0.0 copy-start.3
  1.5 13.2 %all-to-all-start.1 = ((bf16[8,2,2,8,128]{4,3,2,1,0:T(8,128)(2,1)}), bf16[8,2,2,8,128]{4,3,2,1,0:T(8,128)(2,1)S(1)}, u32[]{:S(2)}, u32[]{:S(2)}) async-start(bf16[8,2,2,8,128]{4,3,2,1,0:T(8,128)(2,1)} %copy.13), calls=%async_computation.1 | async-start | bytes 131072 | tf_op jit(solution)/shard_map/all_to_all | solution.py:83
  14.7 0.0 copy-done.3
  14.7 7.9 %collective-permute-start.1 = (bf16[2,32,128]{2,1,0:T(8,128)(2,1)S(1)}, bf16[2,32,128]{2,1,0:T(8,128)(2,1)S(1)}, u32[]{:S(2)}, u32[]{:S(2)}) collective-permute-start(bf16[2,32,128]{2,1,0:T(8,128)(2,1)S(1)} %copy-done.3), channel_id=1, source_target_pairs={{0,64},{1,65},{2,66},{3,67},{4,68},{5,69},{6,70},{7,71},{8,0},{9,1... | collective-permute-start | bytes 49160 | tf_op jit(solution)/shard_map/ppermute | solution.py:81
  22.6 0.7 collective-permute-start
  23.3 0.2 collective-permute-done.1
  23.5 0.0 collective-permute-done
  23.5 0.9 %all-to-all-done.1 = bf16[8,2,2,8,128]{4,3,2,1,0:T(8,128)(2,1)S(1)} async-done(((bf16[8,2,2,8,128]{4,3,2,1,0:T(8,128)(2,1)}), bf16[8,2,2,8,128]{4,3,2,1,0:T(8,128)(2,1)S(1)}, u32[]{:S(2)}, u32[]{:S(2)}) %all-to-all-start.1) | async-done | bytes 65568 | tf_op jit(solution)/shard_map/all_to_all | solution.py:83
  24.4 0.9 %broadcast_in_dim.4 = bf16[16,2,2,32,128]{4,3,2,1,0:T(8,128)(2,1)} broadcast(bf16[2,2,32,128]{3,2,1,0:T(8,128)(2,1)S(1)} %pad_maximum_fusion.1), dimensions={1,2,3,4} | broadcast | bytes 557056 | tf_op jit(solution)/shard_map/broadcast_in_dim | solution.py:85
  25.3 17.2 %all-to-all-start = ((bf16[16,2,2,32,128]{4,3,2,1,0:T(8,128)(2,1)}), bf16[16,2,2,32,128]{4,3,2,1,0:T(8,128)(2,1)S(1)}, u32[]{:S(2)}, u32[]{:S(2)}) async-start(bf16[16,2,2,32,128]{4,3,2,1,0:T(8,128)(2,1)} %broadcast_in_dim.4), calls=%async_computation | async-start | bytes 1048576 | tf_op jit(solution)/shard_map/all_to_all | solution.py:86
  42.6 8.9 %all-to-all-done.own_ref = bf16[16,2,2,32,128]{4,3,2,1,0:T(8,128)(2,1)S(1)} async-done(((bf16[16,2,2,32,128]{4,3,2,1,0:T(8,128)(2,1)}), bf16[16,2,2,32,128]{4,3,2,1,0:T(8,128)(2,1)S(1)}, u32[]{:S(2)}, u32[]{:S(2)}) %all-to-all-start) | async-done | bytes 524320 | tf_op jit(solution)/shard_map/all_to_all | solution.py:86
  51.5 0.0 copy-start
  51.5 0.8 %broadcast_in_dim.5 = bf16[4,8,2,2,8,128]{5,4,1,3,2,0:T(8,128)(2,1)} broadcast(bf16[8,2,2,8,128]{4,3,0,2,1:T(8,128)(2,1)S(1)} %copy.14), dimensions={1,2,3,4,5} | broadcast | bytes 327680 | tf_op jit(solution)/shard_map/broadcast_in_dim | solution.py:87
  52.3 3.4 %all-to-all-start.2 = ((bf16[4,8,2,2,8,128]{5,4,1,3,2,0:T(8,128)(2,1)}), bf16[4,8,2,2,8,128]{5,4,1,3,2,0:T(8,128)(2,1)S(1)}, u32[]{:S(2)}, u32[]{:S(2)}) async-start(bf16[4,8,2,2,8,128]{5,4,1,3,2,0:T(8,128)(2,1)} %broadcast_in_dim.5), calls=%async_computation.2 | async-start | bytes 524288 | tf_op jit(solution)/shard_map/all_to_all | solution.py:88
  55.7 6.0 %collective-permute-start.2 = (bf16[16,2,2,32,128]{4,3,2,1,0:T(8,128)(2,1)S(1)}, bf16[16,2,2,32,128]{4,3,2,1,0:T(8,128)(2,1)S(1)}, u32[]{:S(2)}, u32[]{:S(2)}) collective-permute-start(bf16[16,2,2,32,128]{4,3,2,1,0:T(8,128)(2,1)S(1)} %all-to-all-done.own_ref), channel_id=1, source_target_pairs={{0,1},{1,0},{2,3},{3,2},{4,5},{5,4},{6,7},{7,6},{8,9},{9,8},{10,11... | collective-permute-start | bytes 1572872 | tf_op jit(solution)/shard_map/ppermute | solution.py:91
  61.7 0.0 all-to-all-done.2
  61.8 0.0 copy-start.1
  61.8 0.0 copy-done
  61.8 6.6 %collective-permute-start.3 = (bf16[2,2,256,128]{3,2,1,0:T(8,128)(2,1)S(1)}, bf16[2,2,256,128]{3,2,1,0:T(8,128)(2,1)S(1)}, u32[]{:S(2)}, u32[]{:S(2)}) collective-permute-start(bf16[2,2,256,128]{3,2,1,0:T(8,128)(2,1)S(1)} %bitcast.15), channel_id=1, source_target_pairs={{0,1},{1,0},{2,3},{3,2},{4,5},{5,4},{6,7},{7,6},{8,9},{9,8},{10,11... | collective-permute-start | bytes 786440 | tf_op jit(solution)/shard_map/ppermute | solution.py:92
  68.4 0.0 copy-done.1
  68.4 0.1 reshape.18
  68.6 0.1 stack.21
  68.7 0.1 stack.22
  68.8 0.6 pad_add_fusion.owner_ref
  69.4 0.2 collective-permute-done.3
  69.6 0.9 %pad_maximum_fusion.cont_ref = bf16[2,2,512,128]{3,2,1,0:T(8,128)(2,1)} fusion(bf16[2,2,256,128]{3,2,1,0:T(8,128)(2,1)S(1)} %collective-permute-done.3, bf16[2,2,256,128]{3,2,1,0:T(8,128)(2,1)S(1)} %bitcast.16), kind=kLoop, calls=%fused_computation | loop fusion | flops 1048576 | bytes 1048576 | tf_op jit(solution)/shard_map/concatenate | solution.py:93
  70.4 0.0 collective-permute-done.2.other_ref
  70.4 0.0 copy-start.2
  70.4 0.8 %copy-done.2 = bf16[16,2,2,32,128]{4,3,2,1,0:T(8,128)(2,1)} copy-done((bf16[16,2,2,32,128]{4,3,2,1,0:T(8,128)(2,1)}, bf16[16,2,2,32,128]{4,3,2,1,0:T(8,128)(2,1)S(1)}, u32[]{:S(2)}) %copy-start.2) | copy-done | bytes 524312
  71.2 7.4 %shard_map.64 = bf16[2,512,128]{2,1,0:T(8,128)(2,1)} custom-call(bf16[2,512,128]{2,1,0:T(8,128)(2,1)} %q_ref.1, bf16[16,2,2,32,128]{4,3,2,1,0:T(8,128)(2,1)} %copy-done, bf16[16,2,2,32,128]{4,3,2,1,0:T(8,128)(2,1)} %copy-done.2, bf16[2,2,512,128]{3,2,1,0:T(8,128)(2,1)} %pad_maximum_fusion.cont_ref, s32[2,2,8,128]{3,2,1,0:T(8,128)} %pad_add_fusion.owner_ref, ...), custom_call_target="tpu_custom_call" | custom-call | flops 1400000000 | bytes 3000000 | tf_op jit(solution)/shard_map/pallas_call | solution.py:97
  (6 shorter events, 0.1 us)
Async XLA Ops:
  1.5 13.2 %copy-start.3 = (bf16[2,32,128]{2,1,0:T(8,128)(2,1)S(1)}, bf16[2,32,128]{2,1,0:T(8,128)(2,1)}, u32[]{:S(2)}) copy-start(bf16[2,32,128]{2,1,0:T(8,128)(2,1)} %param.7) | copy-start | bytes 49156
  1.5 22.9 %all-to-all-start.1 = ((bf16[8,2,2,8,128]{4,3,2,1,0:T(8,128)(2,1)}), bf16[8,2,2,8,128]{4,3,2,1,0:T(8,128)(2,1)S(1)}, u32[]{:S(2)}, u32[]{:S(2)}) async-start(bf16[8,2,2,8,128]{4,3,2,1,0:T(8,128)(2,1)} %copy.13), calls=%async_computation.1 | async-start | bytes 131072 | tf_op jit(solution)/shard_map/all_to_all | solution.py:83
  14.7 8.8 %collective-permute-start.1 = (bf16[2,32,128]{2,1,0:T(8,128)(2,1)S(1)}, bf16[2,32,128]{2,1,0:T(8,128)(2,1)S(1)}, u32[]{:S(2)}, u32[]{:S(2)}) collective-permute-start(bf16[2,32,128]{2,1,0:T(8,128)(2,1)S(1)} %copy-done.3), channel_id=1, source_target_pairs={{0,64},{1,65},{2,66},{3,67},{4,68},{5,69},{6,70},{7,71},{8,0},{9,1... | collective-permute-start | bytes 49160 | tf_op jit(solution)/shard_map/ppermute | solution.py:81
  22.6 0.9 %collective-permute-start = (bf16[2,32,128]{2,1,0:T(8,128)(2,1)S(1)}, bf16[2,32,128]{2,1,0:T(8,128)(2,1)S(1)}, u32[]{:S(2)}, u32[]{:S(2)}) collective-permute-start(bf16[2,32,128]{2,1,0:T(8,128)(2,1)S(1)} %copy-done.3), channel_id=1, source_target_pairs={{0,0},{1,1},{2,2},{3,3},{4,4},{5,5},{6,6},{7,7},{8,64},{9,65},{10,... | collective-permute-start | bytes 49160 | tf_op jit(solution)/shard_map/ppermute | solution.py:80
  25.3 26.1 %all-to-all-start = ((bf16[16,2,2,32,128]{4,3,2,1,0:T(8,128)(2,1)}), bf16[16,2,2,32,128]{4,3,2,1,0:T(8,128)(2,1)S(1)}, u32[]{:S(2)}, u32[]{:S(2)}) async-start(bf16[16,2,2,32,128]{4,3,2,1,0:T(8,128)(2,1)} %broadcast_in_dim.4), calls=%async_computation | async-start | bytes 1048576 | tf_op jit(solution)/shard_map/all_to_all | solution.py:86
  51.5 10.3 %copy-start = (bf16[16,2,2,32,128]{4,3,2,1,0:T(8,128)(2,1)}, bf16[16,2,2,32,128]{4,3,2,1,0:T(8,128)(2,1)S(1)}, u32[]{:S(2)}) copy-start(bf16[16,2,2,32,128]{4,3,2,1,0:T(8,128)(2,1)S(1)} %all-to-all-done.own_ref) | copy-start | bytes 1572868
  52.3 9.4 %all-to-all-start.2 = ((bf16[4,8,2,2,8,128]{5,4,1,3,2,0:T(8,128)(2,1)}), bf16[4,8,2,2,8,128]{5,4,1,3,2,0:T(8,128)(2,1)S(1)}, u32[]{:S(2)}, u32[]{:S(2)}) async-start(bf16[4,8,2,2,8,128]{5,4,1,3,2,0:T(8,128)(2,1)} %broadcast_in_dim.5), calls=%async_computation.2 | async-start | bytes 524288 | tf_op jit(solution)/shard_map/all_to_all | solution.py:88
  55.7 14.7 %collective-permute-start.2 = (bf16[16,2,2,32,128]{4,3,2,1,0:T(8,128)(2,1)S(1)}, bf16[16,2,2,32,128]{4,3,2,1,0:T(8,128)(2,1)S(1)}, u32[]{:S(2)}, u32[]{:S(2)}) collective-permute-start(bf16[16,2,2,32,128]{4,3,2,1,0:T(8,128)(2,1)S(1)} %all-to-all-done.own_ref), channel_id=1, source_target_pairs={{0,1},{1,0},{2,3},{3,2},{4,5},{5,4},{6,7},{7,6},{8,9},{9,8},{10,11... | collective-permute-start | bytes 1572872 | tf_op jit(solution)/shard_map/ppermute | solution.py:91
  61.8 6.7 %copy-start.1 = (s32[2048]{0:T(1024)S(1)}, s32[2048]{0:T(1024)}, u32[]{:S(2)}) copy-start(s32[2048]{0:T(1024)} %param.9) | copy-start | bytes 24580
  61.8 7.8 %collective-permute-start.3 = (bf16[2,2,256,128]{3,2,1,0:T(8,128)(2,1)S(1)}, bf16[2,2,256,128]{3,2,1,0:T(8,128)(2,1)S(1)}, u32[]{:S(2)}, u32[]{:S(2)}) collective-permute-start(bf16[2,2,256,128]{3,2,1,0:T(8,128)(2,1)S(1)} %bitcast.15), channel_id=1, source_target_pairs={{0,1},{1,0},{2,3},{3,2},{4,5},{5,4},{6,7},{7,6},{8,9},{9,8},{10,11... | collective-permute-start | bytes 786440 | tf_op jit(solution)/shard_map/ppermute | solution.py:92
  70.4 0.8 %copy-start.2 = (bf16[16,2,2,32,128]{4,3,2,1,0:T(8,128)(2,1)}, bf16[16,2,2,32,128]{4,3,2,1,0:T(8,128)(2,1)S(1)}, u32[]{:S(2)}) copy-start(bf16[16,2,2,32,128]{4,3,2,1,0:T(8,128)(2,1)S(1)} %collective-permute-done.2.other_ref) | copy-start | bytes 1572868

commit v2 on v1

v2 whole, which is shorter than its diff:
```python
import functools
import itertools

import jax
import jax.numpy as jnp
from jax import lax
from jax.experimental import pallas as pl
from jax.experimental.pallas import tpu as pltpu
from jax.sharding import Mesh, PartitionSpec as P


HEAD_SIZE = 128
KEY_VALUE_HEADS = 8
AXES = ("x", "zh", "zl", "y", "c")
DIMS = (4, 2, 8, 4, 2)
NEG = -1e30
FACTOR = HEAD_SIZE**-0.5 * 1.4426950408889634
ROWS = 128
TRANSPOSED = (((1,), (1,)), ((), ()))


def flat(x, zh, zl, y, c):
    return (((x * 2 + zh) * 8 + zl) * 4 + y) * 2 + c


def hops(source, target, size):
    apart = abs(source - target) % size
    return min(apart, size - apart)


def nearest(blocks, head, plane):
    def cost(order):
        lengths = [
            hops(8 * (head % 2) + a, plane, 16) + hops(head // 2, x, 4)
            for a, x in zip(blocks, order)
        ]
        return max(lengths), sum(length * length for length in lengths)

    order = min(itertools.permutations(range(4)), key=cost)
    return cost(order), dict(zip(blocks, order))


def block_plan():
    near, far, slots = {}, {}, []
    for head in range(8):
        best = None
        for low in itertools.combinations(range(8), 4):
            high = tuple(a for a in range(8) if a not in low)
            here = [nearest(low, head, head), nearest(high, head, head + 8)]
            there = [nearest(high, head, head), nearest(low, head, head + 8)]
            cost = (max(h[0] for h in here), max(h[0] for h in there))
            if best is None or cost < best[0]:
                best = (cost, here, there)
        for z in range(2):
            for a, x in best[1][z][1].items():
                near[head, a] = (x, z)
            for a, x in best[2][z][1].items():
                far[head, a] = (x, z)
    for z in range(2):
        for head in range(8):
            packed = 0
            for a in range(8):
                second = near[head, a][1] != z
                x = (far if second else near)[head, a][0]
                packed |= (2 * x + second) << (3 * a)
            slots.append(packed)
    return near, far, slots


NEAR, FAR, SLOTS = block_plan()


def block_moves(plan):
    moves = []
    for (head, a), (x, z) in plan.items():
        for y in range(4):
            for c in range(2):
                moves.append((flat(head // 2, head % 2, a, y, c), flat(x, z, head, y, c)))
    return moves


def first_sample():
    return (lax.axis_index("x") * 2 + lax.axis_index("zh")) * 2


def with_ones(values):
    return jnp.concatenate([values, jnp.ones_like(values)], axis=1)


def weigh(part, top, values):
    wide = jnp.concatenate([top] * (part.shape[1] // HEAD_SIZE), axis=1)
    weights = jnp.exp2((part - wide) * FACTOR).astype(jnp.bfloat16)
    both = jnp.dot(weights, values, preferred_element_type=jnp.float32)
    return both[:, :HEAD_SIZE], both[:, HEAD_SIZE:]


def peak_of(part):
    return jnp.broadcast_to(part.max(axis=1, keepdims=True), (ROWS, HEAD_SIZE))


def split_heads(cont_ref, out_ref):
    for head in range(KEY_VALUE_HEADS):
        piece = cont_ref[:, :, :, head * HEAD_SIZE : (head + 1) * HEAD_SIZE]
        for y in range(4):
            out_ref[head, y] = piece


def repeat_blocks(first_ref, second_ref, out_ref):
    pair = (first_ref[...], second_ref[...])
    for x in range(4):
        for y in range(4):
            for which in range(2):
                out_ref[x, y, which] = pair[which]


TILES = [(here, row) for here in range(2) for row in range(0, 512, ROWS)]


def attend_cont(
    q_ref, near_ref, far_ref, lengths_ref, offsets_ref, owner_ref, top_ref, total_ref, mixed_ref
):
    core = lax.axis_index("c")
    base = first_sample()

    def side(kind, here, row):
        count = (row + ROWS) // 2
        return jnp.concatenate([near_ref[kind, here, :count], far_ref[kind, here, :count]])

    def product(here, row):
        return lax.dot_general(
            q_ref[here, row : row + ROWS],
            side(0, here, row),
            TRANSPOSED,
            preferred_element_type=jnp.float32,
        )

    ahead = product(*TILES[0])
    for index, (here, row) in enumerate(TILES):
        part = ahead
        if index + 1 < len(TILES):
            ahead = product(*TILES[index + 1])
        count = (row + ROWS) // 2
        col = lax.broadcasted_iota(jnp.int32, (1, 2 * count), 1)
        far = col >= count
        col = jnp.where(far, col - count, col)
        u = ((col >> 3) * 2 + jnp.where(far, 1 - core, core)) * 8 + (col & 7)
        t = row + lax.broadcasted_iota(jnp.int32, (ROWS, 1), 0)
        part = jnp.where(u <= jnp.minimum(t, lengths_ref[base + here] - 1), part, NEG)
        top = peak_of(part)
        mixed, total = weigh(part, top, with_ones(side(1, here, row)))
        top_ref[here, row : row + ROWS] = top
        total_ref[here, row : row + ROWS] = total
        mixed_ref[here, row : row + ROWS] = mixed


def attend_prompt(
    last, q_ref, half_ref, owner_ref, lengths_ref, offsets_ref, top_ref, total_ref, mixed_ref, *outs
):
    core = lax.axis_index("c")
    which = 1 - core if last else core
    base = first_sample()
    plane = lax.axis_index("zh") * 8 + lax.axis_index("zl")
    packed = jnp.int32(0)
    for index, slots in enumerate(SLOTS):
        packed = jnp.where(plane == index, jnp.int32(slots), packed)
    keys, values = [], []
    for a in range(8):
        slot = (packed >> (3 * a)) & 7
        keys.append(half_ref[slot >> 1, :, slot & 1, 0].reshape(128, HEAD_SIZE))
        values.append(half_ref[slot >> 1, :, slot & 1, 1].reshape(128, HEAD_SIZE))
    keys = jnp.concatenate(keys)
    values = with_ones(jnp.concatenate(values))
    col = lax.broadcasted_iota(jnp.int32, (1, 1024), 1)
    place = (col >> 5) * 64 + which * 32 + (col & 31)
    owner = owner_ref[which].reshape(1, 1024)
    biases = []
    for here in range(2):
        seen = (owner == 0) | (owner == base + here + 1)
        biases.append(jnp.where(seen & (place < offsets_ref[base + here]), 0.0, NEG))

    def product(here, row):
        return lax.dot_general(
            q_ref[here, row : row + ROWS], keys, TRANSPOSED, preferred_element_type=jnp.float32
        )

    ahead = product(*TILES[0])
    for index, (here, row) in enumerate(TILES):
        part = ahead
        if index + 1 < len(TILES):
            ahead = product(*TILES[index + 1])
        rows = slice(row, row + ROWS)
        part = part + biases[here]
        before = top_ref[here, rows]
        top = jnp.maximum(before, peak_of(part))
        mixed, total = weigh(part, top, values)
        shrink = jnp.exp2((before - top) * FACTOR)
        mixed += mixed_ref[here, rows] * shrink
        total += total_ref[here, rows] * shrink
        if last:
            t = row + lax.broadcasted_iota(jnp.int32, (ROWS, 1), 0)
            mixed = jnp.where(t < lengths_ref[base + here], mixed / total, 0.0)
            outs[0][here, rows] = mixed.astype(jnp.bfloat16)
        else:
            outs[0][here, rows] = top
            outs[1][here, rows] = total
            outs[2][here, rows] = mixed


def call(kernel, out_shape, flops, *operands):
    vmem = pl.BlockSpec(memory_space=pltpu.VMEM)
    smem = pl.BlockSpec(memory_space=pltpu.SMEM)
    return pl.pallas_call(
        kernel,
        out_shape=out_shape,
        in_specs=[smem if operand.ndim == 1 else vmem for operand in operands],
        out_specs=jax.tree.map(lambda _: vmem, out_shape),
        compiler_params=pltpu.CompilerParams(vmem_limit_bytes=24 << 20),
        cost_estimate=pl.CostEstimate(
            flops=flops, transcendentals=flops // 512, bytes_accessed=2000000
        ),
    )(*operands)


def local(queries, prompt, cont, page_owner, cont_lengths, branch_offsets):
    owner = page_owner.reshape(32, 2, 32).transpose(1, 0, 2).reshape(2, 8, 128)
    pieces = call(
        split_heads, jax.ShapeDtypeStruct((8, 4, 2, 2, 8, HEAD_SIZE), cont.dtype), 0, cont
    ).reshape(32, 2, 2, 8, HEAD_SIZE)
    near = lax.all_to_all(pieces, ("zl", "y"), 0, 0, tiled=True)
    first = lax.ppermute(prompt, AXES, block_moves(NEAR))
    second = lax.ppermute(prompt, AXES, block_moves(FAR))
    spread = call(
        repeat_blocks,
        jax.ShapeDtypeStruct((4, 4, 2) + first.shape, first.dtype),
        0,
        first,
        second,
    )
    own = lax.all_to_all(
        spread.reshape((16, 2) + first.shape), ("x", "y"), 0, 0, tiled=True
    ).reshape(spread.shape)
    near = near.transpose(1, 2, 0, 3, 4).reshape(2, 2, 256, HEAD_SIZE)
    swap = [(0, 1), (1, 0)]
    far = lax.ppermute(near, "c", swap)
    wide = jax.ShapeDtypeStruct(queries.shape, jnp.float32)
    state = call(
        attend_cont,
        (wide, wide, wide),
        200000000,
        queries,
        near,
        far,
        cont_lengths,
        branch_offsets,
        owner,
    )
    other = lax.ppermute(own, "c", swap)
    state = call(
        functools.partial(attend_prompt, False),
        (wide, wide, wide),
        550000000,
        queries,
        own,
        owner,
        cont_lengths,
        branch_offsets,
        *state,
    )
    return call(
        functools.partial(attend_prompt, True),
        jax.ShapeDtypeStruct(queries.shape, jnp.bfloat16),
        550000000,
        queries,
        other,
        owner,
        cont_lengths,
        branch_offsets,
        *state,
    )


def solution(mesh):
    fine = Mesh(mesh.devices.reshape(DIMS), AXES)
    sample, ctx = ("x", "zh"), ("zl", "y", "c")
    in_specs = (
        P(sample, None, ctx),
        P(None, ctx, sample),
        P(None, sample, ctx, None),
        P(),
        P(),
        P(),
    )
    return jax.shard_map(
        local, mesh=fine, in_specs=in_specs, out_specs=P(sample, None, ctx), check_vma=False
    )
```

time: 79.2 us -> 82.2 us (1.038)
  waiting for transfers between devices: 10.2 us -> 20.2 us
  local copies, waits for them, and re-layouts: 4.37 us -> 0.24 us
  starting transfers between devices: 55 us -> 52.8 us
  other arithmetic: 1.48 us -> 0 us
  Pallas kernels: 7.4 us -> 8.46 us
    all_to_all x3 -> x2, starting transfers between devices: 33.8 us -> 19.1 us  [the longest x1 9.98 us: local(): lax.all_to_all(spread.reshape((16, 2) + first.shape), ('x', 'y'), 0, 0, t...]
    ppermute x3, starting transfers between devices: 15.2 us -> 28.1 us  [the longest x1 14.4 us: local(): second = lax.ppermute(prompt, AXES, block_moves(FAR))]
    all_to_all x3 -> x2, waiting for transfers between devices: 9.87 us -> 16.7 us  [the longest x1 8.45 us: local(): lax.all_to_all(spread.reshape((16, 2) + first.shape), ('x', 'y'), 0, 0, t...]
    ppermute x3, waiting for transfers between devices: 0.36 us -> 3.5 us  [the longest x1 2.57 us: local(): second = lax.ppermute(prompt, AXES, block_moves(FAR))]
    broadcast_in_dim x2 -> x0, local copies, waits for them, and re-layouts: 1.75 us -> none  [the longest x1 0.91 us: local(): spread = jnp.broadcast_to(pair[None], (16,) + pair.shape)]
    transpose x3 -> x1, local copies, waits for them, and re-layouts: 1.52 us -> 0.01 us  [local(): owner = page_owner.reshape(32, 2, 32).transpose(1, 0, 2).reshape(2, 8, 128)]
    pallas_call x1 -> x5, Pallas kernels: 7.4 us -> 8.46 us  [call(): pl.pallas_call(kernel, out_shape=out_shape, in_specs=[smem if operand.ndi...]
    concatenate x1 -> x0, other arithmetic: 0.86 us -> none  [local(): own_cont = jnp.concatenate([pieces, far], axis=2)]
  transfers between devices with their start and end apart: 7 -> 6, of which waited for: 4 -> 4; matrix products, arithmetic and copies ran while one was open for 2% -> 0% of each run, Pallas kernels for 0% -> 6%
where the time goes in v2:
time: 82.2 us; the launch traced here: 81.8 us
  starting transfers between devices  52.8 us (64%)
  waiting for transfers between devices  20.2 us (25%)
  Pallas kernels  8.46 us (10%)
    ppermute x1, starting transfers between devices, local(): second = lax.ppermute(prompt, AXES, block_moves(FAR))  14.4 us
    all_to_all x1, starting transfers between devices, local(): lax.all_to_all(spread.reshape((16, 2) + first.shape), ('x', 'y'), 0, 0, t...  9.98 us
    all_to_all x1, starting transfers between devices, local(): near = lax.all_to_all(pieces, ('zl', 'y'), 0, 0, tiled=True)  9.14 us
    pallas_call x5, Pallas kernels, call(): pl.pallas_call(kernel, out_shape=out_shape, in_specs=[smem if operand.ndi...  8.46 us
    all_to_all x1, waiting for transfers between devices, local(): lax.all_to_all(spread.reshape((16, 2) + first.shape), ('x', 'y'), 0, 0, t...  8.45 us
    all_to_all x1, waiting for transfers between devices, local(): near = lax.all_to_all(pieces, ('zl', 'y'), 0, 0, tiled=True)  8.27 us
    ppermute x1, starting transfers between devices, local(): far = lax.ppermute(near, 'c', swap)  8.25 us
    ppermute x1, starting transfers between devices, local(): other = lax.ppermute(own, 'c', swap)  5.57 us
  transfers between devices with their start and end apart: 6, of which 4 were waited for; matrix products, arithmetic and copies ran while one was open for 0% of the time, Pallas kernels for 6%

profile of v2, /device:TPU:1, one launch (start us, length us, event | category | flops | bytes accessed | tf_op | source)
XLA Modules:
  0.0 81.8 jit_solution(5192104253112784395)
XLA Ops:
  0.0 5.5 %collective-permute-start = (bf16[2,32,128]{2,1,0:T(8,128)(2,1)}, bf16[2,32,128]{2,1,0:T(8,128)(2,1)S(1)}, u32[]{:S(2)}, u32[]{:S(2)}) collective-permute-start(bf16[2,32,128]{2,1,0:T(8,128)(2,1)} %param.7), channel_id=1, source_target_pairs={{0,256},{1,257},{2,258},{3,259},{4,260},{5,261},{6,262},{7,263},{8... | collective-permute-start | bytes 49160 | tf_op jit(solution)/shard_map/ppermute | solution.py:230
  5.5 14.4 %collective-permute-start.1 = (bf16[2,32,128]{2,1,0:T(8,128)(2,1)}, bf16[2,32,128]{2,1,0:T(8,128)(2,1)S(1)}, u32[]{:S(2)}, u32[]{:S(2)}) collective-permute-start(bf16[2,32,128]{2,1,0:T(8,128)(2,1)} %param.7), channel_id=1, source_target_pairs={{32,256},{33,257},{34,258},{35,259},{36,260},{37,261},{38,262},{39... | collective-permute-start | bytes 49160 | tf_op jit(solution)/shard_map/ppermute | solution.py:231
  19.8 0.0 collective-permute-done.first_ref
  19.8 2.6 %collective-permute-done.1.second_ref = bf16[2,32,128]{2,1,0:T(8,128)(2,1)S(1)} collective-permute-done((bf16[2,32,128]{2,1,0:T(8,128)(2,1)}, bf16[2,32,128]{2,1,0:T(8,128)(2,1)S(1)}, u32[]{:S(2)}, u32[]{:S(2)}) %collective-permute-start.1) | collective-permute-done | bytes 16416 | tf_op jit(solution)/shard_map/ppermute | solution.py:231
  22.4 0.9 %shard_map.64 = bf16[4,4,2,2,32,128]{5,4,3,2,1,0:T(8,128)(2,1)} custom-call(bf16[2,32,128]{2,1,0:T(8,128)(2,1)S(1)} %collective-permute-done.first_ref, bf16[2,32,128]{2,1,0:T(8,128)(2,1)S(1)} %collective-permute-done.1.second_ref), custom_call_target="tpu_custom_call" | custom-call | bytes 2000000 | tf_op jit(solution)/shard_map/pallas_call | solution.py:212
  23.3 0.0 copy-start.1
  23.3 10.0 %all-to-all-start = ((bf16[16,2,2,32,128]{4,3,2,1,0:T(8,128)(2,1)}), bf16[16,2,2,32,128]{4,3,2,1,0:T(8,128)(2,1)S(1)}, u32[]{:S(2)}, u32[]{:S(2)}) async-start(bf16[16,2,2,32,128]{4,3,2,1,0:T(8,128)(2,1)} %bitcast), calls=%async_computation | async-start | bytes 1048576 | tf_op jit(solution)/shard_map/all_to_all | solution.py:239
  33.3 0.0 copy-done.1
  33.3 0.7 shard_map.65
  34.1 8.4 %all-to-all-done = bf16[16,2,2,32,128]{4,3,2,1,0:T(8,128)(2,1)S(1)} async-done(((bf16[16,2,2,32,128]{4,3,2,1,0:T(8,128)(2,1)}), bf16[16,2,2,32,128]{4,3,2,1,0:T(8,128)(2,1)S(1)}, u32[]{:S(2)}, u32[]{:S(2)}) %all-to-all-start) | async-done | bytes 524320 | tf_op jit(solution)/shard_map/all_to_all | solution.py:239
  42.5 9.1 %all-to-all-start.1 = ((bf16[32,2,2,8,128]{4,3,2,1,0:T(8,128)(2,1)}), bf16[32,2,2,8,128]{4,3,2,1,0:T(8,128)(2,1)S(1)}, u32[]{:S(2)}, u32[]{:S(2)}) async-start(bf16[32,2,2,8,128]{4,3,2,1,0:T(8,128)(2,1)} %bitcast.3), calls=%async_computation.1 | async-start | bytes 524288 | tf_op jit(solution)/shard_map/all_to_all | solution.py:229
  51.6 0.0 copy-start.4
  51.7 0.0 copy-start
  51.7 5.6 %collective-permute-start.2 = (bf16[4,4,2,2,32,128]{5,4,3,2,1,0:T(8,128)(2,1)S(1)}, bf16[4,4,2,2,32,128]{5,4,3,2,1,0:T(8,128)(2,1)S(1)}, u32[]{:S(2)}, u32[]{:S(2)}) collective-permute-start(bf16[4,4,2,2,32,128]{5,4,3,2,1,0:T(8,128)(2,1)S(1)} %bitcast.9), channel_id=1, source_target_pairs={{0,1},{1,0},{2,3},{3,2},{4,5},{5,4},{6,7},{7,6},{8,9},{9,8},{10,11... | collective-permute-start | bytes 1572872 | tf_op jit(solution)/shard_map/ppermute | solution.py:257
  57.2 8.3 %all-to-all-done.1 = bf16[32,2,2,8,128]{4,3,2,1,0:T(8,128)(2,1)S(1)} async-done(((bf16[32,2,2,8,128]{4,3,2,1,0:T(8,128)(2,1)}), bf16[32,2,2,8,128]{4,3,2,1,0:T(8,128)(2,1)S(1)}, u32[]{:S(2)}, u32[]{:S(2)}) %all-to-all-start.1) | async-done | bytes 262176 | tf_op jit(solution)/shard_map/all_to_all | solution.py:229
  65.6 8.2 %collective-permute-start.3 = (bf16[2,2,256,128]{3,2,1,0:T(8,128)(2,1)S(1)}, bf16[2,2,256,128]{3,2,1,0:T(8,128)(2,1)S(1)}, u32[]{:S(2)}, u32[]{:S(2)}) collective-permute-start(bf16[2,2,256,128]{3,2,1,0:T(8,128)(2,1)S(1)} %copy_bitcast_fusion.near_ref), channel_id=1, source_target_pairs={{0,1},{1,0},{2,3},{3,2},{4,5},{5,4},{6,7},{7,6},{8,9},{9,8},{10,11... | collective-permute-start | bytes 786440 | tf_op jit(solution)/shard_map/ppermute | solution.py:244
  73.8 0.0 copy-done.4
  73.8 0.1 reshape.20
  73.9 0.0 copy-start.2
  74.0 0.0 copy-start.3
  74.0 0.1 reshape.21.owner_ref
  74.0 0.9 %collective-permute-done.3.far_ref = bf16[2,2,256,128]{3,2,1,0:T(8,128)(2,1)S(1)} collective-permute-done((bf16[2,2,256,128]{3,2,1,0:T(8,128)(2,1)S(1)}, bf16[2,2,256,128]{3,2,1,0:T(8,128)(2,1)S(1)}, u32[]{:S(2)}, u32[]{:S(2)}) %collective-permute-start.3) | collective-permute-done | bytes 262176 | tf_op jit(solution)/shard_map/ppermute | solution.py:244
  75.0 0.0 copy-done
  75.0 0.0 copy-done.2
  75.0 0.0 copy-done.3
  75.0 1.7 %shard_map.66 = (f32[2,512,128]{2,1,0:T(8,128)S(1)}, f32[2,512,128]{2,1,0:T(8,128)S(1)}, f32[2,512,128]{2,1,0:T(8,128)S(1)}) custom-call(bf16[2,512,128]{2,1,0:T(8,128)(2,1)S(1)} %copy-done, bf16[2,2,256,128]{3,2,1,0:T(8,128)(2,1)S(1)} %copy_bitcast_fusion.near_ref, bf16[2,2,256,128]{3,2,1,0:T(8,128)(2,1)S(1)} %collective-permute-done.3.far_ref, ...), custom_call_target="tpu_custom_call" | custom-call | flops 200000000 | bytes 2000000 | tf_op jit(solution)/shard_map/pallas_call | solution.py:212
  76.7 2.2 %shard_map.67 = (f32[2,512,128]{2,1,0:T(8,128)S(1)}, f32[2,512,128]{2,1,0:T(8,128)S(1)}, f32[2,512,128]{2,1,0:T(8,128)S(1)}) custom-call(bf16[2,512,128]{2,1,0:T(8,128)(2,1)S(1)} %copy-done, bf16[4,4,2,2,32,128]{5,4,3,2,1,0:T(8,128)(2,1)S(1)} %bitcast.10, s32[2,8,128]{2,1,0:T(8,128)S(1)} %reshape.21.owner_ref, s32[16]{0:T(128)S(1)} %copy-done.2, ...), custom_call_target="tpu_custom_call" | custom-call | flops 550000000 | bytes 2000000 | tf_op jit(solution)/shard_map/pallas_call | solution.py:212
  78.9 0.0 collective-permute-done.2.half_ref
  78.9 2.9 %shard_map.68 = bf16[2,512,128]{2,1,0:T(8,128)(2,1)} custom-call(bf16[2,512,128]{2,1,0:T(8,128)(2,1)S(1)} %copy-done, bf16[4,4,2,2,32,128]{5,4,3,2,1,0:T(8,128)(2,1)S(1)} %collective-permute-done.2.half_ref, s32[2,8,128]{2,1,0:T(8,128)S(1)} %reshape.21.owner_ref, s32[16]{0:T(128)S(1)} %copy-done.2, s32[16]{0:T(128)S(1)} %copy-done.3, ...), custom_call_target="tpu_custom_call" | custom-call | flops 550000000 | bytes 2000000 | tf_op jit(solution)/shard_map/pallas_call | solution.py:212
  (2 shorter events, 0.1 us)
Async XLA Ops:
  0.0 19.8 %collective-permute-start = (bf16[2,32,128]{2,1,0:T(8,128)(2,1)}, bf16[2,32,128]{2,1,0:T(8,128)(2,1)S(1)}, u32[]{:S(2)}, u32[]{:S(2)}) collective-permute-start(bf16[2,32,128]{2,1,0:T(8,128)(2,1)} %param.7), channel_id=1, source_target_pairs={{0,256},{1,257},{2,258},{3,259},{4,260},{5,261},{6,262},{7,263},{8... | collective-permute-start | bytes 49160 | tf_op jit(solution)/shard_map/ppermute | solution.py:230
  5.5 16.9 %collective-permute-start.1 = (bf16[2,32,128]{2,1,0:T(8,128)(2,1)}, bf16[2,32,128]{2,1,0:T(8,128)(2,1)S(1)}, u32[]{:S(2)}, u32[]{:S(2)}) collective-permute-start(bf16[2,32,128]{2,1,0:T(8,128)(2,1)} %param.7), channel_id=1, source_target_pairs={{32,256},{33,257},{34,258},{35,259},{36,260},{37,261},{38,262},{39... | collective-permute-start | bytes 49160 | tf_op jit(solution)/shard_map/ppermute | solution.py:231
  23.3 10.0 %copy-start.1 = (bf16[2,2,8,1024]{3,2,1,0:T(8,128)(2,1)S(1)}, bf16[2,2,8,1024]{3,2,1,0:T(8,128)(2,1)}, u32[]{:S(2)}) copy-start(bf16[2,2,8,1024]{3,2,1,0:T(8,128)(2,1)} %cont_ref.1) | copy-start | bytes 196612
  23.3 19.2 %all-to-all-start = ((bf16[16,2,2,32,128]{4,3,2,1,0:T(8,128)(2,1)}), bf16[16,2,2,32,128]{4,3,2,1,0:T(8,128)(2,1)S(1)}, u32[]{:S(2)}, u32[]{:S(2)}) async-start(bf16[16,2,2,32,128]{4,3,2,1,0:T(8,128)(2,1)} %bitcast), calls=%async_computation | async-start | bytes 1048576 | tf_op jit(solution)/shard_map/all_to_all | solution.py:239
  42.5 23.0 %all-to-all-start.1 = ((bf16[32,2,2,8,128]{4,3,2,1,0:T(8,128)(2,1)}), bf16[32,2,2,8,128]{4,3,2,1,0:T(8,128)(2,1)S(1)}, u32[]{:S(2)}, u32[]{:S(2)}) async-start(bf16[32,2,2,8,128]{4,3,2,1,0:T(8,128)(2,1)} %bitcast.3), calls=%async_computation.1 | async-start | bytes 524288 | tf_op jit(solution)/shard_map/all_to_all | solution.py:229
  51.6 22.2 %copy-start.4 = (s32[2048]{0:T(1024)S(1)}, s32[2048]{0:T(1024)}, u32[]{:S(2)}) copy-start(s32[2048]{0:T(1024)} %param.9) | copy-start | bytes 24580
  51.7 23.3 %copy-start = (bf16[2,512,128]{2,1,0:T(8,128)(2,1)S(1)}, bf16[2,512,128]{2,1,0:T(8,128)(2,1)}, u32[]{:S(2)}) copy-start(bf16[2,512,128]{2,1,0:T(8,128)(2,1)} %q_ref.5) | copy-start | bytes 786436
  51.7 27.2 %collective-permute-start.2 = (bf16[4,4,2,2,32,128]{5,4,3,2,1,0:T(8,128)(2,1)S(1)}, bf16[4,4,2,2,32,128]{5,4,3,2,1,0:T(8,128)(2,1)S(1)}, u32[]{:S(2)}, u32[]{:S(2)}) collective-permute-start(bf16[4,4,2,2,32,128]{5,4,3,2,1,0:T(8,128)(2,1)S(1)} %bitcast.9), channel_id=1, source_target_pairs={{0,1},{1,0},{2,3},{3,2},{4,5},{5,4},{6,7},{7,6},{8,9},{9,8},{10,11... | collective-permute-start | bytes 1572872 | tf_op jit(solution)/shard_map/ppermute | solution.py:257
  65.6 9.4 %collective-permute-start.3 = (bf16[2,2,256,128]{3,2,1,0:T(8,128)(2,1)S(1)}, bf16[2,2,256,128]{3,2,1,0:T(8,128)(2,1)S(1)}, u32[]{:S(2)}, u32[]{:S(2)}) collective-permute-start(bf16[2,2,256,128]{3,2,1,0:T(8,128)(2,1)S(1)} %copy_bitcast_fusion.near_ref), channel_id=1, source_target_pairs={{0,1},{1,0},{2,3},{3,2},{4,5},{5,4},{6,7},{7,6},{8,9},{9,8},{10,11... | collective-permute-start | bytes 786440 | tf_op jit(solution)/shard_map/ppermute | solution.py:244
  73.9 1.0 %copy-start.2 = (s32[16]{0:T(128)S(1)}, s32[16]{0:T(128)}, u32[]{:S(2)}) copy-start(s32[16]{0:T(128)} %lengths_ref.5) | copy-start | bytes 196
  74.0 1.0 %copy-start.3 = (s32[16]{0:T(128)S(1)}, s32[16]{0:T(128)}, u32[]{:S(2)}) copy-start(s32[16]{0:T(128)} %offsets_ref.5) | copy-start | bytes 196

commit v3 on v2

v3 whole, which is shorter than its diff:
```python
import jax
import jax.numpy as jnp
from jax import lax
from jax.experimental import pallas as pl
from jax.experimental.pallas import tpu as pltpu
from jax.sharding import Mesh, PartitionSpec as P


HEAD_SIZE = 128
KEY_VALUE_HEADS = 8
AXES = ("x", "zh", "zl", "y", "c")
DIMS = (4, 2, 8, 4, 2)
NEG = -1e30
FACTOR = HEAD_SIZE**-0.5 * 1.4426950408889634
ROWS = 128
TRANSPOSED = (((1,), (1,)), ((), ()))


def flat(x, zh, zl, y, c):
    return (((x * 2 + zh) * 8 + zl) * 4 + y) * 2 + c


def hops(source, target, size):
    apart = abs(source - target) % size
    return min(apart, size - apart)


def block_plan():
    plan, chunks = {}, []
    for z in range(2):
        for head in range(8):
            places = [(x, c) for x in range(4) for c in range(2)]
            places.sort(key=lambda place: hops(head // 2, place[0], 4))
            blocks = sorted(range(8), key=lambda a: -hops(8 * (head % 2) + a, head + 8 * z, 16))
            packed = 0
            for a, (x, c) in zip(blocks, places):
                plan[z, head, a] = (x, c)
                packed |= a << (12 * c + 3 * x)
            chunks.append(packed)
    return plan, chunks


PLAN, CHUNKS = block_plan()


def block_moves():
    moves = []
    for (z, head, a), (x, c) in PLAN.items():
        for y in range(4):
            moves.append((flat(head // 2, head % 2, a, y, z), flat(x, z, head, y, c)))
    return moves


def first_sample():
    return (lax.axis_index("x") * 2 + lax.axis_index("zh")) * 2


def with_ones(values):
    return jnp.concatenate([values, jnp.ones_like(values)], axis=1)


def weigh(part, top, values):
    wide = jnp.concatenate([top] * (part.shape[1] // HEAD_SIZE), axis=1)
    weights = jnp.exp2((part - wide) * FACTOR).astype(jnp.bfloat16)
    both = jnp.dot(weights, values, preferred_element_type=jnp.float32)
    return both[:, :HEAD_SIZE], both[:, HEAD_SIZE:]


def peak_of(part):
    return jnp.broadcast_to(part.max(axis=1, keepdims=True), (ROWS, HEAD_SIZE))


def split_heads(cont_ref, out_ref):
    for head in range(KEY_VALUE_HEADS):
        piece = cont_ref[:, :, :, head * HEAD_SIZE : (head + 1) * HEAD_SIZE]
        for core in range(2):
            out_ref[head, core] = piece


def repeat_blocks(pair_ref, out_ref):
    pair = pair_ref[...]
    for x in range(4):
        for y in range(4):
            out_ref[x, y] = pair


TILES = [(here, row) for here in range(2) for row in range(0, 512, ROWS)]


def prompt_half(half_ref):
    keys = half_ref[:, :, :, 0].reshape(1024, HEAD_SIZE)
    return keys, with_ones(half_ref[:, :, :, 1].reshape(1024, HEAD_SIZE))


def prompt_biases(which, owner_ref, offsets_ref):
    base = first_sample()
    plane = lax.axis_index("zh") * 8 + lax.axis_index("zl")
    packed = jnp.int32(0)
    for index, chunks in enumerate(CHUNKS):
        packed = jnp.where(plane == index, jnp.int32(chunks), packed)
    col = lax.broadcasted_iota(jnp.int32, (1, 256), 1)
    owners, places = [], []
    for x in range(4):
        chunk = (packed >> (12 * which + 3 * x)) & 7
        owner = owner_ref[chunk]
        owners += [owner[0:1], owner[1:2]]
        places.append(chunk * 256 + col)
    owner = jnp.concatenate(owners, axis=1)
    place = jnp.concatenate(places, axis=1)
    biases = []
    for here in range(2):
        seen = (owner == 0) | (owner == base + here + 1)
        biases.append(jnp.where(seen & (place < offsets_ref[base + here]), 0.0, NEG))
    return biases


def scores(q, keys):
    return lax.dot_general(q, keys, TRANSPOSED, preferred_element_type=jnp.float32)


def attend_own(
    q_ref, half_ref, owner_ref, lengths_ref, offsets_ref, top_ref, total_ref, mixed_ref
):
    keys, values = prompt_half(half_ref)
    biases = prompt_biases(lax.axis_index("c"), owner_ref, offsets_ref)

    def product(here, row):
        return scores(q_ref[here, row : row + ROWS], keys)

    ahead = product(*TILES[0])
    for index, (here, row) in enumerate(TILES):
        part = ahead
        if index + 1 < len(TILES):
            ahead = product(*TILES[index + 1])
        rows = slice(row, row + ROWS)
        part = part + biases[here]
        top = peak_of(part)
        mixed, total = weigh(part, top, values)
        top_ref[here, rows] = top
        total_ref[here, rows] = total
        mixed_ref[here, rows] = mixed


def attend_rest(
    q_ref,
    half_ref,
    near_ref,
    far_ref,
    owner_ref,
    lengths_ref,
    offsets_ref,
    top_ref,
    total_ref,
    mixed_ref,
    out_ref,
):
    base = first_sample()
    keys, values = prompt_half(half_ref)
    biases = prompt_biases(1 - lax.axis_index("c"), owner_ref, offsets_ref)

    def side(kind, here, row):
        count = (row + ROWS) // 4
        return jnp.concatenate(
            [ref[kind, here, k, :count] for ref in (near_ref, far_ref) for k in range(2)]
        )

    def product(here, row):
        q = q_ref[here, row : row + ROWS]
        return scores(q, keys), scores(q, side(0, here, row))

    ahead = product(*TILES[0])
    for index, (here, row) in enumerate(TILES):
        part, cont = ahead
        if index + 1 < len(TILES):
            ahead = product(*TILES[index + 1])
        rows = slice(row, row + ROWS)
        part = part + biases[here]
        count = (row + ROWS) // 4
        col = lax.broadcasted_iota(jnp.int32, (1, 4 * count), 1)
        step = (col >= count).astype(jnp.int32)
        step += (col >= 2 * count).astype(jnp.int32) + (col >= 3 * count).astype(jnp.int32)
        col = col - step * count
        y = lax.axis_index("y") ^ step ^ (step >> 1)
        u = (col >> 4) * 64 + y * 16 + (col & 15)
        t = row + lax.broadcasted_iota(jnp.int32, (ROWS, 1), 0)
        length = lengths_ref[base + here]
        cont = jnp.where(u <= jnp.minimum(t, length - 1), cont, NEG)
        before = top_ref[here, rows]
        top = jnp.maximum(before, jnp.maximum(peak_of(part), peak_of(cont)))
        mixed, total = weigh(part, top, values)
        more = weigh(cont, top, with_ones(side(1, here, row)))
        shrink = jnp.exp2((before - top) * FACTOR)
        mixed += more[0] + mixed_ref[here, rows] * shrink
        total += more[1] + total_ref[here, rows] * shrink
        out_ref[here, rows] = jnp.where(t < length, mixed / total, 0.0).astype(jnp.bfloat16)


def call(kernel, out_shape, flops, *operands):
    vmem = pl.BlockSpec(memory_space=pltpu.VMEM)
    smem = pl.BlockSpec(memory_space=pltpu.SMEM)
    return pl.pallas_call(
        kernel,
        out_shape=out_shape,
        in_specs=[smem if operand.ndim == 1 else vmem for operand in operands],
        out_specs=jax.tree.map(lambda _: vmem, out_shape),
        compiler_params=pltpu.CompilerParams(vmem_limit_bytes=24 << 20),
        cost_estimate=pl.CostEstimate(
            flops=flops, transcendentals=flops // 512, bytes_accessed=2000000
        ),
    )(*operands)


def local(queries, prompt, cont, page_owner, cont_lengths, branch_offsets):
    owner = page_owner.reshape(8, 2, 128)
    pieces = call(
        split_heads, jax.ShapeDtypeStruct((8, 2, 2, 2, 8, HEAD_SIZE), cont.dtype), 0, cont
    ).reshape(16, 2, 2, 8, HEAD_SIZE)
    mine = lax.all_to_all(pieces, ("zl", "c"), 0, 0, tiled=True)
    pair = lax.all_gather(prompt, "c")
    pair = lax.ppermute(pair, AXES, block_moves())
    spread = call(repeat_blocks, jax.ShapeDtypeStruct((4, 4) + pair.shape, pair.dtype), 0, pair)
    own = lax.all_to_all(
        spread.reshape((16,) + pair.shape), ("x", "y"), 0, 0, tiled=True
    ).reshape(spread.shape)
    beside = lax.ppermute(mine, "y", [(0, 1), (1, 0), (2, 3), (3, 2)])
    near = jnp.stack([mine, beside]).transpose(2, 3, 0, 1, 4, 5)
    near = near.reshape(2, 2, 2, 128, HEAD_SIZE)
    far = lax.ppermute(near, "y", [(0, 3), (3, 0), (1, 2), (2, 1)])
    other = lax.ppermute(own, "c", [(0, 1), (1, 0)])
    wide = jax.ShapeDtypeStruct(queries.shape, jnp.float32)
    state = call(
        attend_own,
        (wide, wide, wide),
        550000000,
        queries,
        own,
        owner,
        cont_lengths,
        branch_offsets,
    )
    return call(
        attend_rest,
        jax.ShapeDtypeStruct(queries.shape, jnp.bfloat16),
        750000000,
        queries,
        other,
        near,
        far,
        owner,
        cont_lengths,
        branch_offsets,
        *state,
    )


def solution(mesh):
    fine = Mesh(mesh.devices.reshape(DIMS), AXES)
    sample, ctx = ("x", "zh"), ("zl", "y", "c")
    in_specs = (
        P(sample, None, ctx),
        P(None, ctx, sample),
        P(None, sample, ctx, None),
        P(),
        P(),
        P(),
    )
    return jax.shard_map(
        local, mesh=fine, in_specs=in_specs, out_specs=P(sample, None, ctx), check_vma=False
    )
```

time: 82.2 us -> 82.4 us (level)
  starting transfers between devices: 52.8 us -> 34.9 us
  waiting for transfers between devices: 20.2 us -> 30.4 us
  blocking collectives: 0 us -> 8.52 us
    ppermute x4, starting transfers between devices: 33.6 us -> 16.8 us  [the longest x1 10.3 us: local(): pair = lax.ppermute(pair, AXES, block_moves())]
    all_gather x0 -> x1, blocking collectives: none -> 8.52 us  [local(): pair = lax.all_gather(prompt, 'c')]
    ppermute x4, waiting for transfers between devices: 3.5 us -> 10.9 us  [the longest x1 5.45 us: local(): far = lax.ppermute(near, 'y', [(0, 3), (3, 0), (1, 2), (2, 1)])]
    all_to_all x2, waiting for transfers between devices: 16.7 us -> 19.5 us  [the longest x1 9.97 us: local(): mine = lax.all_to_all(pieces, ('zl', 'c'), 0, 0, tiled=True)]
    all_to_all x2, starting transfers between devices: 19.1 us -> 18.1 us  [the longest x1 13.7 us: local(): mine = lax.all_to_all(pieces, ('zl', 'c'), 0, 0, tiled=True)]
    pallas_call x5 -> x4, Pallas kernels: 8.46 us -> 8 us  [call(): pl.pallas_call(kernel, out_shape=out_shape, in_specs=[smem if operand.ndi...]
  transfers between devices with their start and end apart: 6 -> 6, of which waited for: 4 -> 5; matrix products, arithmetic and copies ran while one was open for 0% -> 0% of each run, Pallas kernels for 6% -> 3%
where the time goes in v3:
time: 82.4 us; the launch traced here: 82 us
  starting transfers between devices  34.9 us (42%)
  waiting for transfers between devices  30.4 us (37%)
  blocking collectives  8.52 us (10%)
  Pallas kernels  8 us (10%)
    all_to_all x1, starting transfers between devices, local(): mine = lax.all_to_all(pieces, ('zl', 'c'), 0, 0, tiled=True)  13.7 us
    ppermute x1, starting transfers between devices, local(): pair = lax.ppermute(pair, AXES, block_moves())  10.3 us
    all_to_all x1, waiting for transfers between devices, local(): mine = lax.all_to_all(pieces, ('zl', 'c'), 0, 0, tiled=True)  9.97 us
    all_to_all x1, waiting for transfers between devices, local(): lax.all_to_all(spread.reshape((16,) + pair.shape), ('x', 'y'), 0, 0, tile...  9.5 us
    all_gather x1, blocking collectives, local(): pair = lax.all_gather(prompt, 'c')  8.52 us
    pallas_call x4, Pallas kernels, call(): pl.pallas_call(kernel, out_shape=out_shape, in_specs=[smem if operand.ndi...  8 us
    ppermute x1, waiting for transfers between devices, local(): far = lax.ppermute(near, 'y', [(0, 3), (3, 0), (1, 2), (2, 1)])  5.45 us
    ppermute x1, waiting for transfers between devices, local(): beside = lax.ppermute(mine, 'y', [(0, 1), (1, 0), (2, 3), (3, 2)])  4.47 us
  transfers between devices with their start and end apart: 6, of which 5 were waited for; matrix products, arithmetic and copies ran while one was open for 0% of the time, Pallas kernels for 3%

profile of v3, /device:TPU:1, one launch (start us, length us, event | category | flops | bytes accessed | tf_op | source)
XLA Modules:
  0.0 82.0 jit_solution(10538863669431169980)
XLA Ops:
  0.0 8.5 %all-gather = bf16[4,32,128]{2,1,0:T(8,128)(2,1)S(1)} all-gather(bf16[2,32,128]{2,1,0:T(8,128)(2,1)} %param.7), channel_id=2, replica_groups=mesh['x'=4,'zh'=2,'zl'=8,'y'=4,'c'=2] {'c'}, dimensions={0}, use_global_device_ids=true | all-gather | bytes 49152 | tf_op jit(solution)/shard_map/all_gather | solution.py:219
  8.5 10.3 %collective-permute-start = (bf16[2,2,32,128]{3,2,1,0:T(8,128)(2,1)S(1)}, bf16[2,2,32,128]{3,2,1,0:T(8,128)(2,1)S(1)}, u32[]{:S(2)}, u32[]{:S(2)}) collective-permute-start(bf16[2,2,32,128]{3,2,1,0:T(8,128)(2,1)S(1)} %bitcast.18), channel_id=1, source_target_pairs={{56,0},{58,2},{60,4},{62,6},{48,1},{50,3},{52,5},{54,7},{40,128},{... | collective-permute-start | bytes 98312 | tf_op jit(solution)/shard_map/ppermute | solution.py:220
  18.8 1.0 %collective-permute-done.pair_ref = bf16[2,2,32,128]{3,2,1,0:T(8,128)(2,1)S(1)} collective-permute-done((bf16[2,2,32,128]{3,2,1,0:T(8,128)(2,1)S(1)}, bf16[2,2,32,128]{3,2,1,0:T(8,128)(2,1)S(1)}, u32[]{:S(2)}, u32[]{:S(2)}) %collective-permute-start) | collective-permute-done | bytes 32800 | tf_op jit(solution)/shard_map/ppermute | solution.py:220
  19.9 0.9 %shard_map.64 = bf16[4,4,2,2,32,128]{5,4,3,2,1,0:T(8,128)(2,1)} custom-call(bf16[2,2,32,128]{3,2,1,0:T(8,128)(2,1)S(1)} %collective-permute-done.pair_ref), custom_call_target="tpu_custom_call" | custom-call | bytes 2000000 | tf_op jit(solution)/shard_map/pallas_call | solution.py:201
  20.7 0.0 copy-start.1
  20.8 4.4 %all-to-all-start = ((bf16[16,2,2,32,128]{4,3,2,1,0:T(8,128)(2,1)}), bf16[16,2,2,32,128]{4,3,2,1,0:T(8,128)(2,1)S(1)}, u32[]{:S(2)}, u32[]{:S(2)}) async-start(bf16[16,2,2,32,128]{4,3,2,1,0:T(8,128)(2,1)} %bitcast.1), calls=%async_computation | async-start | bytes 1048576 | tf_op jit(solution)/shard_map/all_to_all | solution.py:222
  25.2 0.0 copy-done.1
  25.2 0.7 shard_map.65
  25.9 9.5 %all-to-all-done = bf16[16,2,2,32,128]{4,3,2,1,0:T(8,128)(2,1)S(1)} async-done(((bf16[16,2,2,32,128]{4,3,2,1,0:T(8,128)(2,1)}), bf16[16,2,2,32,128]{4,3,2,1,0:T(8,128)(2,1)S(1)}, u32[]{:S(2)}, u32[]{:S(2)}) %all-to-all-start) | async-done | bytes 524320 | tf_op jit(solution)/shard_map/all_to_all | solution.py:222
  35.4 13.7 %all-to-all-start.1 = ((bf16[16,2,2,8,128]{4,3,2,1,0:T(8,128)(2,1)}), bf16[16,2,2,8,128]{4,3,2,1,0:T(8,128)(2,1)S(1)}, u32[]{:S(2)}, u32[]{:S(2)}) async-start(bf16[16,2,2,8,128]{4,3,2,1,0:T(8,128)(2,1)} %bitcast.3), calls=%async_computation.1 | async-start | bytes 262144 | tf_op jit(solution)/shard_map/all_to_all | solution.py:218
  49.0 2.0 %collective-permute-start.1 = (bf16[4,4,2,2,32,128]{5,4,3,2,1,0:T(8,128)(2,1)S(1)}, bf16[4,4,2,2,32,128]{5,4,3,2,1,0:T(8,128)(2,1)S(1)}, u32[]{:S(2)}, u32[]{:S(2)}) collective-permute-start(bf16[4,4,2,2,32,128]{5,4,3,2,1,0:T(8,128)(2,1)S(1)} %bitcast.12), channel_id=1, source_target_pairs={{0,1},{1,0},{2,3},{3,2},{4,5},{5,4},{6,7},{7,6},{8,9},{9,8},{10,11... | collective-permute-start | bytes 1572872 | tf_op jit(solution)/shard_map/ppermute | solution.py:229
  51.1 10.0 %all-to-all-done.1 = bf16[16,2,2,8,128]{4,3,2,1,0:T(8,128)(2,1)S(1)} async-done(((bf16[16,2,2,8,128]{4,3,2,1,0:T(8,128)(2,1)}), bf16[16,2,2,8,128]{4,3,2,1,0:T(8,128)(2,1)S(1)}, u32[]{:S(2)}, u32[]{:S(2)}) %all-to-all-start.1) | async-done | bytes 131104 | tf_op jit(solution)/shard_map/all_to_all | solution.py:218
  61.0 2.2 %collective-permute-start.2 = (bf16[16,2,2,8,128]{4,3,2,1,0:T(8,128)(2,1)S(1)}, bf16[16,2,2,8,128]{4,3,2,1,0:T(8,128)(2,1)S(1)}, u32[]{:S(2)}, u32[]{:S(2)}) collective-permute-start(bf16[16,2,2,8,128]{4,3,2,1,0:T(8,128)(2,1)S(1)} %all-to-all-done.1), channel_id=1, source_target_pairs={{0,2},{2,0},{4,6},{6,4},{1,3},{3,1},{5,7},{7,5},{8,10},{10,8},{12,... | collective-permute-start | bytes 393224 | tf_op jit(solution)/shard_map/ppermute | solution.py:225
  63.2 4.5 %collective-permute-done.2 = bf16[16,2,2,8,128]{4,3,2,1,0:T(8,128)(2,1)S(1)} collective-permute-done((bf16[16,2,2,8,128]{4,3,2,1,0:T(8,128)(2,1)S(1)}, bf16[16,2,2,8,128]{4,3,2,1,0:T(8,128)(2,1)S(1)}, u32[]{:S(2)}, u32[]{:S(2)}) %collective-permute-start.2) | collective-permute-done | bytes 131104 | tf_op jit(solution)/shard_map/ppermute | solution.py:225
  67.7 0.0 copy-start
  67.7 0.0 copy-start.2
  67.7 0.0 copy-start.3
  67.8 0.0 copy-start.4
  67.8 2.3 %collective-permute-start.3 = (bf16[2,2,2,128,128]{4,3,2,1,0:T(8,128)(2,1)S(1)}, bf16[2,2,2,128,128]{4,3,2,1,0:T(8,128)(2,1)S(1)}, u32[]{:S(2)}, u32[]{:S(2)}) collective-permute-start(bf16[2,2,2,128,128]{4,3,2,1,0:T(8,128)(2,1)S(1)} %copy_bitcast_fusion.near_ref), channel_id=1, source_target_pairs={{0,6},{6,0},{2,4},{4,2},{1,7},{7,1},{3,5},{5,3},{8,14},{14,8},{10,... | collective-permute-start | bytes 786440 | tf_op jit(solution)/shard_map/ppermute | solution.py:228
  70.1 0.0 copy-done
  70.1 0.0 copy-done.2
  70.1 0.0 copy-done.3
  70.1 0.0 copy-done.4
  70.1 2.1 %shard_map.66 = (f32[2,512,128]{2,1,0:T(8,128)S(1)}, f32[2,512,128]{2,1,0:T(8,128)S(1)}, f32[2,512,128]{2,1,0:T(8,128)S(1)}) custom-call(bf16[2,512,128]{2,1,0:T(8,128)(2,1)S(1)} %copy-done, bf16[4,4,2,2,32,128]{5,4,3,2,1,0:T(8,128)(2,1)S(1)} %bitcast.13, s32[8,2,128]{2,1,0:T(2,128)S(1)} %bitcast.14, s32[16]{0:T(128)S(1)} %copy-done.3, s32[16]{0:T(128)S(1)} %copy-done.4), custom_call_target="tpu_custom_call" | custom-call | flops 550000000 | bytes 2000000 | tf_op jit(solution)/shard_map/pallas_call | solution.py:201
  72.3 5.5 %collective-permute-done.3.far_ref = bf16[2,2,2,128,128]{4,3,2,1,0:T(8,128)(2,1)S(1)} collective-permute-done((bf16[2,2,2,128,128]{4,3,2,1,0:T(8,128)(2,1)S(1)}, bf16[2,2,2,128,128]{4,3,2,1,0:T(8,128)(2,1)S(1)}, u32[]{:S(2)}, u32[]{:S(2)}) %collective-permute-start.3) | collective-permute-done | bytes 262176 | tf_op jit(solution)/shard_map/ppermute | solution.py:228
  77.7 0.0 collective-permute-done.1.half_ref
  77.7 4.3 %shard_map.67 = bf16[2,512,128]{2,1,0:T(8,128)(2,1)} custom-call(bf16[2,512,128]{2,1,0:T(8,128)(2,1)S(1)} %copy-done, bf16[4,4,2,2,32,128]{5,4,3,2,1,0:T(8,128)(2,1)S(1)} %collective-permute-done.1.half_ref, bf16[2,2,2,128,128]{4,3,2,1,0:T(8,128)(2,1)S(1)} %copy_bitcast_fusion.near_ref, bf16[2,2,2,128,128]{4,3,2,1,0:T(8,128)(2,1)S(1)} %collective-permute-done.3.far_ref, ...), custom_call_target="tpu_custom_call" | custom-call | flops 750000000 | bytes 2000000 | tf_op jit(solution)/shard_map/pallas_call | solution.py:201
  (1 shorter events, 0.0 us)
Async XLA Ops:
  8.5 11.3 %collective-permute-start = (bf16[2,2,32,128]{3,2,1,0:T(8,128)(2,1)S(1)}, bf16[2,2,32,128]{3,2,1,0:T(8,128)(2,1)S(1)}, u32[]{:S(2)}, u32[]{:S(2)}) collective-permute-start(bf16[2,2,32,128]{3,2,1,0:T(8,128)(2,1)S(1)} %bitcast.18), channel_id=1, source_target_pairs={{56,0},{58,2},{60,4},{62,6},{48,1},{50,3},{52,5},{54,7},{40,128},{... | collective-permute-start | bytes 98312 | tf_op jit(solution)/shard_map/ppermute | solution.py:220
  20.7 4.4 %copy-start.1 = (bf16[2,2,8,1024]{3,2,1,0:T(8,128)(2,1)S(1)}, bf16[2,2,8,1024]{3,2,1,0:T(8,128)(2,1)}, u32[]{:S(2)}) copy-start(bf16[2,2,8,1024]{3,2,1,0:T(8,128)(2,1)} %cont_ref.1) | copy-start | bytes 196612
  20.8 14.6 %all-to-all-start = ((bf16[16,2,2,32,128]{4,3,2,1,0:T(8,128)(2,1)}), bf16[16,2,2,32,128]{4,3,2,1,0:T(8,128)(2,1)S(1)}, u32[]{:S(2)}, u32[]{:S(2)}) async-start(bf16[16,2,2,32,128]{4,3,2,1,0:T(8,128)(2,1)} %bitcast.1), calls=%async_computation | async-start | bytes 1048576 | tf_op jit(solution)/shard_map/all_to_all | solution.py:222
  35.4 25.7 %all-to-all-start.1 = ((bf16[16,2,2,8,128]{4,3,2,1,0:T(8,128)(2,1)}), bf16[16,2,2,8,128]{4,3,2,1,0:T(8,128)(2,1)S(1)}, u32[]{:S(2)}, u32[]{:S(2)}) async-start(bf16[16,2,2,8,128]{4,3,2,1,0:T(8,128)(2,1)} %bitcast.3), calls=%async_computation.1 | async-start | bytes 262144 | tf_op jit(solution)/shard_map/all_to_all | solution.py:218
  49.0 28.7 %collective-permute-start.1 = (bf16[4,4,2,2,32,128]{5,4,3,2,1,0:T(8,128)(2,1)S(1)}, bf16[4,4,2,2,32,128]{5,4,3,2,1,0:T(8,128)(2,1)S(1)}, u32[]{:S(2)}, u32[]{:S(2)}) collective-permute-start(bf16[4,4,2,2,32,128]{5,4,3,2,1,0:T(8,128)(2,1)S(1)} %bitcast.12), channel_id=1, source_target_pairs={{0,1},{1,0},{2,3},{3,2},{4,5},{5,4},{6,7},{7,6},{8,9},{9,8},{10,11... | collective-permute-start | bytes 1572872 | tf_op jit(solution)/shard_map/ppermute | solution.py:229
  61.0 6.7 %collective-permute-start.2 = (bf16[16,2,2,8,128]{4,3,2,1,0:T(8,128)(2,1)S(1)}, bf16[16,2,2,8,128]{4,3,2,1,0:T(8,128)(2,1)S(1)}, u32[]{:S(2)}, u32[]{:S(2)}) collective-permute-start(bf16[16,2,2,8,128]{4,3,2,1,0:T(8,128)(2,1)S(1)} %all-to-all-done.1), channel_id=1, source_target_pairs={{0,2},{2,0},{4,6},{6,4},{1,3},{3,1},{5,7},{7,5},{8,10},{10,8},{12,... | collective-permute-start | bytes 393224 | tf_op jit(solution)/shard_map/ppermute | solution.py:225
  67.7 2.4 %copy-start = (bf16[2,512,128]{2,1,0:T(8,128)(2,1)S(1)}, bf16[2,512,128]{2,1,0:T(8,128)(2,1)}, u32[]{:S(2)}) copy-start(bf16[2,512,128]{2,1,0:T(8,128)(2,1)} %q_ref.3) | copy-start | bytes 786436
  67.7 2.4 %copy-start.2 = (s32[2048]{0:T(1024)S(1)}, s32[2048]{0:T(1024)}, u32[]{:S(2)}) copy-start(s32[2048]{0:T(1024)} %param.9) | copy-start | bytes 24580
  67.7 2.4 %copy-start.3 = (s32[16]{0:T(128)S(1)}, s32[16]{0:T(128)}, u32[]{:S(2)}) copy-start(s32[16]{0:T(128)} %lengths_ref.3) | copy-start | bytes 196
  67.8 2.4 %copy-start.4 = (s32[16]{0:T(128)S(1)}, s32[16]{0:T(128)}, u32[]{:S(2)}) copy-start(s32[16]{0:T(128)} %offsets_ref.3) | copy-start | bytes 196
  67.8 10.0 %collective-permute-start.3 = (bf16[2,2,2,128,128]{4,3,2,1,0:T(8,128)(2,1)S(1)}, bf16[2,2,2,128,128]{4,3,2,1,0:T(8,128)(2,1)S(1)}, u32[]{:S(2)}, u32[]{:S(2)}) collective-permute-start(bf16[2,2,2,128,128]{4,3,2,1,0:T(8,128)(2,1)S(1)} %copy_bitcast_fusion.near_ref), channel_id=1, source_target_pairs={{0,6},{6,0},{2,4},{4,2},{1,7},{7,1},{3,5},{5,3},{8,14},{14,8},{10,... | collective-permute-start | bytes 786440 | tf_op jit(solution)/shard_map/ppermute | solution.py:228

commit v4 on v3

--- a/solution.py
+++ b/solution.py
@@ -84,12 +84,42 @@
             out_ref[x, y] = pair
 
 
-TILES = [(here, row) for here in range(2) for row in range(0, 512, ROWS)]
-
-
-def prompt_half(half_ref):
-    keys = half_ref[:, :, :, 0].reshape(1024, HEAD_SIZE)
-    return keys, with_ones(half_ref[:, :, :, 1].reshape(1024, HEAD_SIZE))
+def run_tiles(tiles, product, consume):
+    ahead = product(*tiles[0])
+    for index, tile in enumerate(tiles):
+        part = ahead
+        if index + 1 < len(tiles):
+            ahead = product(*tiles[index + 1])
+        consume(*tile, part)
+
+
+def live_rows(lengths_ref, product, consume, blank=None):
+    base = first_sample()
+    run_tiles([(here, row) for here in range(2) for row in (0, ROWS)], product, consume)
+    for here in range(2):
+        length = lengths_ref[base + here]
+        tiles = [(here, 2 * ROWS), (here, 3 * ROWS)]
+
+        @pl.when(length > 3 * ROWS)
+        def _():
+            run_tiles(tiles, product, consume)
+
+        @pl.when((length > 2 * ROWS) & (length <= 3 * ROWS))
+        def _():
+            run_tiles(tiles[:1], product, consume)
+            if blank is not None:
+                blank(*tiles[1])
+
+        if blank is not None:
+
+            @pl.when(length <= 2 * ROWS)
+            def _():
+                for tile in tiles:
+                    blank(*tile)
+
+
+def prompt_side(half_ref, kind):
+    return half_ref[:, :, :, kind].reshape(1024, HEAD_SIZE)
 
 
 def prompt_biases(which, owner_ref, offsets_ref):
@@ -118,33 +148,76 @@
     return lax.dot_general(q, keys, TRANSPOSED, preferred_element_type=jnp.float32)
 
 
+def cont_side(ref, kind, here, row):
+    count = 64 if row < 2 * ROWS else 128
+    return jnp.concatenate([ref[kind, here, 0, :count], ref[kind, here, 1, :count]])
+
+
+def cont_mask(cont, far, row, length):
+    count = cont.shape[1] // 2
+    col = lax.broadcasted_iota(jnp.int32, (1, 2 * count), 1)
+    step = (col >= count).astype(jnp.int32)
+    col = col - step * count
+    y = lax.axis_index("y") ^ step ^ (3 if far else 0)
+    u = (col >> 4) * 64 + y * 16 + (col & 15)
+    t = row + lax.broadcasted_iota(jnp.int32, (ROWS, 1), 0)
+    return jnp.where(u <= jnp.minimum(t, length - 1), cont, NEG)
+
+
+def attend_near(
+    q_ref, near_ref, lengths_ref, offsets_ref, owner_ref, top_ref, total_ref, mixed_ref
+):
+    base = first_sample()
+
+    def product(here, row):
+        return scores(q_ref[here, row : row + ROWS], cont_side(near_ref, 0, here, row))
+
+    def consume(here, row, cont):
+        cont = cont_mask(cont, False, row, lengths_ref[base + here])
+        top = peak_of(cont)
+        mixed, total = weigh(cont, top, with_ones(cont_side(near_ref, 1, here, row)))
+        top_ref[here, row : row + ROWS] = top
+        total_ref[here, row : row + ROWS] = total
+        mixed_ref[here, row : row + ROWS] = mixed
+
+    live_rows(lengths_ref, product, consume)
+
+
 def attend_own(
-    q_ref, half_ref, owner_ref, lengths_ref, offsets_ref, top_ref, total_ref, mixed_ref
+    q_ref,
+    half_ref,
+    owner_ref,
+    lengths_ref,
+    offsets_ref,
+    top_ref,
+    total_ref,
+    mixed_ref,
+    top_out,
+    total_out,
+    mixed_out,
 ):
-    keys, values = prompt_half(half_ref)
     biases = prompt_biases(lax.axis_index("c"), owner_ref, offsets_ref)
 
     def product(here, row):
-        return scores(q_ref[here, row : row + ROWS], keys)
-
-    ahead = product(*TILES[0])
-    for index, (here, row) in enumerate(TILES):
-        part = ahead
-        if index + 1 < len(TILES):
-            ahead = product(*TILES[index + 1])
+        return scores(q_ref[here, row : row + ROWS], prompt_side(half_ref, 0))
+
+    def consume(here, row, part):
         rows = slice(row, row + ROWS)
         part = part + biases[here]
-        top = peak_of(part)
-        mixed, total = weigh(part, top, values)
-        top_ref[here, rows] = top
-        total_ref[here, rows] = total
-        mixed_ref[here, rows] = mixed
+        before = top_ref[here, rows]
+        top = jnp.maximum(before, peak_of(part))
+        mixed, total = weigh(part, top, with_ones(prompt_side(half_ref, 1)))
+        shrink = jnp.exp2((before - top) * FACTOR)
+        top_out[here, rows] = top
+        total_out[here, rows] = total + total_ref[here, rows] * shrink
+        mixed_out[here, rows] = mixed + mixed_ref[here, rows] * shrink
+
+    live_rows(lengths_ref, product, consume)
 
 
 def attend_rest(
     q_ref,
     half_ref,
-    near_ref,
     far_ref,
     owner_ref,
     lengths_ref,
@@ -155,44 +228,31 @@
     out_ref,
 ):
     base = first_sample()
-    keys, values = prompt_half(half_ref)
     biases = prompt_biases(1 - lax.axis_index("c"), owner_ref, offsets_ref)
-
-    def side(kind, here, row):
-        count = (row + ROWS) // 4
-        return jnp.concatenate(
-            [ref[kind, here, k, :count] for ref in (near_ref, far_ref) for k in range(2)]
-        )
 
     def product(here, row):
         q = q_ref[here, row : row + ROWS]
-        return scores(q, keys), scores(q, side(0, here, row))
-
-    ahead = product(*TILES[0])
-    for index, (here, row) in enumerate(TILES):
-        part, cont = ahead
-        if index + 1 < len(TILES):
-            ahead = product(*TILES[index + 1])
+        return scores(q, prompt_side(half_ref, 0)), scores(q, cont_side(far_ref, 0, here, row))
+
+    def consume(here, row, parts):
         rows = slice(row, row + ROWS)
-        part = part + biases[here]
-        count = (row + ROWS) // 4
-        col = lax.broadcasted_iota(jnp.int32, (1, 4 * count), 1)
-        step = (col >= count).astype(jnp.int32)
-        step += (col >= 2 * count).astype(jnp.int32) + (col >= 3 * count).astype(jnp.int32)
-        col = col - step * count
-        y = lax.axis_index("y") ^ step ^ (step >> 1)
-        u = (col >> 4) * 64 + y * 16 + (col & 15)
-        t = row + lax.broadcasted_iota(jnp.int32, (ROWS, 1), 0)
         length = lengths_ref[base + here]
-        cont = jnp.where(u <= jnp.minimum(t, length - 1), cont, NEG)
+        part = parts[0] + biases[here]
+        cont = cont_mask(parts[1], True, row, length)
         before = top_ref[here, rows]
         top = jnp.maximum(before, jnp.maximum(peak_of(part), peak_of(cont)))
-        mixed, total = weigh(part, top, values)
-        more = weigh(cont, top, with_ones(side(1, here, row)))
+        mixed, total = weigh(part, top, with_ones(prompt_side(half_ref, 1)))
+        more = weigh(cont, top, with_ones(cont_side(far_ref, 1, here, row)))
         shrink = jnp.exp2((before - top) * FACTOR)
         mixed += more[0] + mixed_ref[here, rows] * shrink
         total += more[1] + total_ref[here, rows] * shrink
+        t = row + lax.broadcasted_iota(jnp.int32, (ROWS, 1), 0)
         out_ref[here, rows] = jnp.where(t < length, mixed / total, 0.0).astype(jnp.bfloat16)
+
+    def blank(here, row):
+        out_ref[here, row : row + ROWS] = jnp.zeros((ROWS, HEAD_SIZE), jnp.bfloat16)
+
+    live_rows(lengths_ref, product, consume, blank)
 
 
 def call(kernel, out_shape, flops, *operands):
@@ -218,7 +278,9 @@
     mine = lax.all_to_all(pieces, ("zl", "c"), 0, 0, tiled=True)
     pair = lax.all_gather(prompt, "c")
     pair = lax.ppermute(pair, AXES, block_moves())
-    spread = call(repeat_blocks, jax.ShapeDtypeStruct((4, 4) + pair.shape, pair.dtype), 0, pair)
+    spread = call(
+        repeat_blocks, jax.ShapeDtypeStruct((4, 4) + pair.shape, pair.dtype), 0, pair
+    )
     own = lax.all_to_all(
         spread.reshape((16,) + pair.shape), ("x", "y"), 0, 0, tiled=True
     ).reshape(spread.shape)
@@ -229,6 +291,16 @@
     other = lax.ppermute(own, "c", [(0, 1), (1, 0)])
     wide = jax.ShapeDtypeStruct(queries.shape, jnp.float32)
     state = call(
+        attend_near,
+        (wide, wide, wide),
+        100000000,
+        queries,
+        near,
+        cont_lengths,
+        branch_offsets,
+        owner,
+    )
+    state = call(
         attend_own,
         (wide, wide, wide),
         550000000,
@@ -237,14 +309,14 @@
         owner,
         cont_lengths,
         branch_offsets,
+        *state,
     )
     return call(
         attend_rest,
         jax.ShapeDtypeStruct(queries.shape, jnp.bfloat16),
-        750000000,
+        650000000,
         queries,
         other,
-        near,
         far,
         owner,
         cont_lengths,

time: 82.4 us -> 81.9 us (level)
  waiting for transfers between devices: 30.4 us -> 28 us
  Pallas kernels: 8 us -> 9.81 us
    ppermute x1, waiting for transfers between devices: 5.45 us -> 3.04 us  [local(): far = lax.ppermute(near, 'y', [(0, 3), (3, 0), (1, 2), (2, 1)])]
    pallas_call x4 -> x5, Pallas kernels: 8 us -> 9.81 us  [call(): pl.pallas_call(kernel, out_shape=out_shape, in_specs=[smem if operand.ndi...]
  transfers between devices with their start and end apart: 6 -> 6, of which waited for: 5 -> 5; matrix products, arithmetic and copies ran while one was open for 0% -> 0% of each run, Pallas kernels for 3% -> 6%
where the time goes in v4:
time: 81.9 us; the launch traced here: 81.4 us
  starting transfers between devices  34.9 us (43%)
  waiting for transfers between devices  28 us (34%)
  Pallas kernels  9.81 us (12%)
  blocking collectives  8.52 us (10%)
    all_to_all x1, starting transfers between devices, local(): mine = lax.all_to_all(pieces, ('zl', 'c'), 0, 0, tiled=True)  13.7 us
    ppermute x1, starting transfers between devices, local(): pair = lax.ppermute(pair, AXES, block_moves())  10.3 us
    all_to_all x1, waiting for transfers between devices, local(): mine = lax.all_to_all(pieces, ('zl', 'c'), 0, 0, tiled=True)  9.97 us
    pallas_call x5, Pallas kernels, call(): pl.pallas_call(kernel, out_shape=out_shape, in_specs=[smem if operand.ndi...  9.81 us
    all_to_all x1, waiting for transfers between devices, local(): lax.all_to_all(spread.reshape((16,) + pair.shape), ('x', 'y'), 0, 0, tile...  9.5 us
    all_gather x1, blocking collectives, local(): pair = lax.all_gather(prompt, 'c')  8.52 us
    ppermute x1, waiting for transfers between devices, local(): beside = lax.ppermute(mine, 'y', [(0, 1), (1, 0), (2, 3), (3, 2)])  4.47 us
    all_to_all x1, starting transfers between devices, local(): lax.all_to_all(spread.reshape((16,) + pair.shape), ('x', 'y'), 0, 0, tile...  4.43 us
  transfers between devices with their start and end apart: 6, of which 5 were waited for; matrix products, arithmetic and copies ran while one was open for 0% of the time, Pallas kernels for 6%

profile of v4, /device:TPU:1, one launch (start us, length us, event | category | flops | bytes accessed | tf_op | source)
XLA Modules:
  0.0 81.4 jit_solution(13208728528904698896)
XLA Ops:
  0.0 8.5 %all-gather = bf16[4,32,128]{2,1,0:T(8,128)(2,1)S(1)} all-gather(bf16[2,32,128]{2,1,0:T(8,128)(2,1)} %param.7), channel_id=2, replica_groups=mesh['x'=4,'zh'=2,'zl'=8,'y'=4,'c'=2] {'c'}, dimensions={0}, use_global_device_ids=true | all-gather | bytes 49152 | tf_op jit(solution)/shard_map/all_gather | solution.py:279
  8.5 10.3 %collective-permute-start = (bf16[2,2,32,128]{3,2,1,0:T(8,128)(2,1)S(1)}, bf16[2,2,32,128]{3,2,1,0:T(8,128)(2,1)S(1)}, u32[]{:S(2)}, u32[]{:S(2)}) collective-permute-start(bf16[2,2,32,128]{3,2,1,0:T(8,128)(2,1)S(1)} %bitcast.19), channel_id=1, source_target_pairs={{56,0},{58,2},{60,4},{62,6},{48,1},{50,3},{52,5},{54,7},{40,128},{... | collective-permute-start | bytes 98312 | tf_op jit(solution)/shard_map/ppermute | solution.py:280
  18.8 1.0 %collective-permute-done.pair_ref = bf16[2,2,32,128]{3,2,1,0:T(8,128)(2,1)S(1)} collective-permute-done((bf16[2,2,32,128]{3,2,1,0:T(8,128)(2,1)S(1)}, bf16[2,2,32,128]{3,2,1,0:T(8,128)(2,1)S(1)}, u32[]{:S(2)}, u32[]{:S(2)}) %collective-permute-start) | collective-permute-done | bytes 32800 | tf_op jit(solution)/shard_map/ppermute | solution.py:280
  19.9 0.9 %shard_map.64 = bf16[4,4,2,2,32,128]{5,4,3,2,1,0:T(8,128)(2,1)} custom-call(bf16[2,2,32,128]{3,2,1,0:T(8,128)(2,1)S(1)} %collective-permute-done.pair_ref), custom_call_target="tpu_custom_call" | custom-call | bytes 2000000 | tf_op jit(solution)/shard_map/pallas_call | solution.py:261
  20.7 0.0 copy-start.2
  20.7 4.4 %all-to-all-start = ((bf16[16,2,2,32,128]{4,3,2,1,0:T(8,128)(2,1)}), bf16[16,2,2,32,128]{4,3,2,1,0:T(8,128)(2,1)S(1)}, u32[]{:S(2)}, u32[]{:S(2)}) async-start(bf16[16,2,2,32,128]{4,3,2,1,0:T(8,128)(2,1)} %bitcast.1), calls=%async_computation | async-start | bytes 1048576 | tf_op jit(solution)/shard_map/all_to_all | solution.py:284
  25.2 0.0 copy-done.2
  25.2 0.7 shard_map.65
  25.9 9.5 %all-to-all-done = bf16[16,2,2,32,128]{4,3,2,1,0:T(8,128)(2,1)S(1)} async-done(((bf16[16,2,2,32,128]{4,3,2,1,0:T(8,128)(2,1)}), bf16[16,2,2,32,128]{4,3,2,1,0:T(8,128)(2,1)S(1)}, u32[]{:S(2)}, u32[]{:S(2)}) %all-to-all-start) | async-done | bytes 524320 | tf_op jit(solution)/shard_map/all_to_all | solution.py:284
  35.4 13.7 %all-to-all-start.1 = ((bf16[16,2,2,8,128]{4,3,2,1,0:T(8,128)(2,1)}), bf16[16,2,2,8,128]{4,3,2,1,0:T(8,128)(2,1)S(1)}, u32[]{:S(2)}, u32[]{:S(2)}) async-start(bf16[16,2,2,8,128]{4,3,2,1,0:T(8,128)(2,1)} %bitcast.3), calls=%async_computation.1 | async-start | bytes 262144 | tf_op jit(solution)/shard_map/all_to_all | solution.py:278
  49.0 2.0 %collective-permute-start.1 = (bf16[4,4,2,2,32,128]{5,4,3,2,1,0:T(8,128)(2,1)S(1)}, bf16[4,4,2,2,32,128]{5,4,3,2,1,0:T(8,128)(2,1)S(1)}, u32[]{:S(2)}, u32[]{:S(2)}) collective-permute-start(bf16[4,4,2,2,32,128]{5,4,3,2,1,0:T(8,128)(2,1)S(1)} %bitcast.12), channel_id=1, source_target_pairs={{0,1},{1,0},{2,3},{3,2},{4,5},{5,4},{6,7},{7,6},{8,9},{9,8},{10,11... | collective-permute-start | bytes 1572872 | tf_op jit(solution)/shard_map/ppermute | solution.py:291
  51.0 10.0 %all-to-all-done.1 = bf16[16,2,2,8,128]{4,3,2,1,0:T(8,128)(2,1)S(1)} async-done(((bf16[16,2,2,8,128]{4,3,2,1,0:T(8,128)(2,1)}), bf16[16,2,2,8,128]{4,3,2,1,0:T(8,128)(2,1)S(1)}, u32[]{:S(2)}, u32[]{:S(2)}) %all-to-all-start.1) | async-done | bytes 131104 | tf_op jit(solution)/shard_map/all_to_all | solution.py:278
  61.0 2.2 %collective-permute-start.2 = (bf16[16,2,2,8,128]{4,3,2,1,0:T(8,128)(2,1)S(1)}, bf16[16,2,2,8,128]{4,3,2,1,0:T(8,128)(2,1)S(1)}, u32[]{:S(2)}, u32[]{:S(2)}) collective-permute-start(bf16[16,2,2,8,128]{4,3,2,1,0:T(8,128)(2,1)S(1)} %all-to-all-done.1), channel_id=1, source_target_pairs={{0,2},{2,0},{4,6},{6,4},{1,3},{3,1},{5,7},{7,5},{8,10},{10,8},{12,... | collective-permute-start | bytes 393224 | tf_op jit(solution)/shard_map/ppermute | solution.py:287
  63.2 4.5 %collective-permute-done.2 = bf16[16,2,2,8,128]{4,3,2,1,0:T(8,128)(2,1)S(1)} collective-permute-done((bf16[16,2,2,8,128]{4,3,2,1,0:T(8,128)(2,1)S(1)}, bf16[16,2,2,8,128]{4,3,2,1,0:T(8,128)(2,1)S(1)}, u32[]{:S(2)}, u32[]{:S(2)}) %collective-permute-start.2) | collective-permute-done | bytes 131104 | tf_op jit(solution)/shard_map/ppermute | solution.py:287
  67.7 0.0 copy-start
  67.7 0.0 copy-start.1
  67.7 0.0 copy-start.3
  67.7 0.0 copy-start.4
  67.8 2.3 %collective-permute-start.3 = (bf16[2,2,2,128,128]{4,3,2,1,0:T(8,128)(2,1)S(1)}, bf16[2,2,2,128,128]{4,3,2,1,0:T(8,128)(2,1)S(1)}, u32[]{:S(2)}, u32[]{:S(2)}) collective-permute-start(bf16[2,2,2,128,128]{4,3,2,1,0:T(8,128)(2,1)S(1)} %copy_bitcast_fusion.near_ref), channel_id=1, source_target_pairs={{0,6},{6,0},{2,4},{4,2},{1,7},{7,1},{3,5},{5,3},{8,14},{14,8},{10,... | collective-permute-start | bytes 786440 | tf_op jit(solution)/shard_map/ppermute | solution.py:290
  70.1 0.0 copy-done
  70.1 0.0 copy-done.1
  70.1 0.0 copy-done.3
  70.1 0.0 copy-done.4
  70.1 1.8 %shard_map.66 = (f32[2,512,128]{2,1,0:T(8,128)S(1)}, f32[2,512,128]{2,1,0:T(8,128)S(1)}, f32[2,512,128]{2,1,0:T(8,128)S(1)}) custom-call(bf16[2,512,128]{2,1,0:T(8,128)(2,1)S(1)} %copy-done, bf16[2,2,2,128,128]{4,3,2,1,0:T(8,128)(2,1)S(1)} %copy_bitcast_fusion.near_ref, s32[16]{0:T(128)S(1)} %copy-done.3, s32[16]{0:T(128)S(1)} %copy-done.4, ...), custom_call_target="tpu_custom_call" | custom-call | flops 100000000 | bytes 2000000 | tf_op jit(solution)/shard_map/pallas_call | solution.py:261
  71.9 2.8 %shard_map.67 = (f32[2,512,128]{2,1,0:T(8,128)S(1)}, f32[2,512,128]{2,1,0:T(8,128)S(1)}, f32[2,512,128]{2,1,0:T(8,128)S(1)}) custom-call(bf16[2,512,128]{2,1,0:T(8,128)(2,1)S(1)} %copy-done, bf16[4,4,2,2,32,128]{5,4,3,2,1,0:T(8,128)(2,1)S(1)} %bitcast.13, s32[8,2,128]{2,1,0:T(2,128)S(1)} %bitcast.15, s32[16]{0:T(128)S(1)} %copy-done.3, s32[16]{0:T(128)S(1)} %copy-done.4, ...), custom_call_target="tpu_custom_call" | custom-call | flops 550000000 | bytes 2000000 | tf_op jit(solution)/shard_map/pallas_call | solution.py:261
  74.7 3.0 %collective-permute-done.3.far_ref = bf16[2,2,2,128,128]{4,3,2,1,0:T(8,128)(2,1)S(1)} collective-permute-done((bf16[2,2,2,128,128]{4,3,2,1,0:T(8,128)(2,1)S(1)}, bf16[2,2,2,128,128]{4,3,2,1,0:T(8,128)(2,1)S(1)}, u32[]{:S(2)}, u32[]{:S(2)}) %collective-permute-start.3) | collective-permute-done | bytes 262176 | tf_op jit(solution)/shard_map/ppermute | solution.py:290
  77.7 0.0 collective-permute-done.1.half_ref
  77.7 3.7 %shard_map.68 = bf16[2,512,128]{2,1,0:T(8,128)(2,1)} custom-call(bf16[2,512,128]{2,1,0:T(8,128)(2,1)S(1)} %copy-done, bf16[4,4,2,2,32,128]{5,4,3,2,1,0:T(8,128)(2,1)S(1)} %collective-permute-done.1.half_ref, bf16[2,2,2,128,128]{4,3,2,1,0:T(8,128)(2,1)S(1)} %collective-permute-done.3.far_ref, s32[8,2,128]{2,1,0:T(2,128)S(1)} %bitcast.16, s32[16]{0:T(128)S(1)} %copy-done.3, ...), custom_call_target="tpu_custom_call" | custom-call | flops 650000000 | bytes 2000000 | tf_op jit(solution)/shard_map/pallas_call | solution.py:261
  (1 shorter events, 0.0 us)
Async XLA Ops:
  8.5 11.3 %collective-permute-start = (bf16[2,2,32,128]{3,2,1,0:T(8,128)(2,1)S(1)}, bf16[2,2,32,128]{3,2,1,0:T(8,128)(2,1)S(1)}, u32[]{:S(2)}, u32[]{:S(2)}) collective-permute-start(bf16[2,2,32,128]{3,2,1,0:T(8,128)(2,1)S(1)} %bitcast.19), channel_id=1, source_target_pairs={{56,0},{58,2},{60,4},{62,6},{48,1},{50,3},{52,5},{54,7},{40,128},{... | collective-permute-start | bytes 98312 | tf_op jit(solution)/shard_map/ppermute | solution.py:280
  20.7 4.4 %copy-start.2 = (bf16[2,2,8,1024]{3,2,1,0:T(8,128)(2,1)S(1)}, bf16[2,2,8,1024]{3,2,1,0:T(8,128)(2,1)}, u32[]{:S(2)}) copy-start(bf16[2,2,8,1024]{3,2,1,0:T(8,128)(2,1)} %cont_ref.1) | copy-start | bytes 196612
  20.7 14.6 %all-to-all-start = ((bf16[16,2,2,32,128]{4,3,2,1,0:T(8,128)(2,1)}), bf16[16,2,2,32,128]{4,3,2,1,0:T(8,128)(2,1)S(1)}, u32[]{:S(2)}, u32[]{:S(2)}) async-start(bf16[16,2,2,32,128]{4,3,2,1,0:T(8,128)(2,1)} %bitcast.1), calls=%async_computation | async-start | bytes 1048576 | tf_op jit(solution)/shard_map/all_to_all | solution.py:284
  35.4 25.7 %all-to-all-start.1 = ((bf16[16,2,2,8,128]{4,3,2,1,0:T(8,128)(2,1)}), bf16[16,2,2,8,128]{4,3,2,1,0:T(8,128)(2,1)S(1)}, u32[]{:S(2)}, u32[]{:S(2)}) async-start(bf16[16,2,2,8,128]{4,3,2,1,0:T(8,128)(2,1)} %bitcast.3), calls=%async_computation.1 | async-start | bytes 262144 | tf_op jit(solution)/shard_map/all_to_all | solution.py:278
  49.0 28.7 %collective-permute-start.1 = (bf16[4,4,2,2,32,128]{5,4,3,2,1,0:T(8,128)(2,1)S(1)}, bf16[4,4,2,2,32,128]{5,4,3,2,1,0:T(8,128)(2,1)S(1)}, u32[]{:S(2)}, u32[]{:S(2)}) collective-permute-start(bf16[4,4,2,2,32,128]{5,4,3,2,1,0:T(8,128)(2,1)S(1)} %bitcast.12), channel_id=1, source_target_pairs={{0,1},{1,0},{2,3},{3,2},{4,5},{5,4},{6,7},{7,6},{8,9},{9,8},{10,11... | collective-permute-start | bytes 1572872 | tf_op jit(solution)/shard_map/ppermute | solution.py:291
  61.0 6.7 %collective-permute-start.2 = (bf16[16,2,2,8,128]{4,3,2,1,0:T(8,128)(2,1)S(1)}, bf16[16,2,2,8,128]{4,3,2,1,0:T(8,128)(2,1)S(1)}, u32[]{:S(2)}, u32[]{:S(2)}) collective-permute-start(bf16[16,2,2,8,128]{4,3,2,1,0:T(8,128)(2,1)S(1)} %all-to-all-done.1), channel_id=1, source_target_pairs={{0,2},{2,0},{4,6},{6,4},{1,3},{3,1},{5,7},{7,5},{8,10},{10,8},{12,... | collective-permute-start | bytes 393224 | tf_op jit(solution)/shard_map/ppermute | solution.py:287
  67.7 2.4 %copy-start = (bf16[2,512,128]{2,1,0:T(8,128)(2,1)S(1)}, bf16[2,512,128]{2,1,0:T(8,128)(2,1)}, u32[]{:S(2)}) copy-start(bf16[2,512,128]{2,1,0:T(8,128)(2,1)} %q_ref.5) | copy-start | bytes 786436
  67.7 2.4 %copy-start.1 = (s32[2048]{0:T(1024)S(1)}, s32[2048]{0:T(1024)}, u32[]{:S(2)}) copy-start(s32[2048]{0:T(1024)} %param.9) | copy-start | bytes 24580
  67.7 2.4 %copy-start.3 = (s32[16]{0:T(128)S(1)}, s32[16]{0:T(128)}, u32[]{:S(2)}) copy-start(s32[16]{0:T(128)} %lengths_ref.5) | copy-start | bytes 196
  67.7 2.4 %copy-start.4 = (s32[16]{0:T(128)S(1)}, s32[16]{0:T(128)}, u32[]{:S(2)}) copy-start(s32[16]{0:T(128)} %offsets_ref.5) | copy-start | bytes 196
  67.8 10.0 %collective-permute-start.3 = (bf16[2,2,2,128,128]{4,3,2,1,0:T(8,128)(2,1)S(1)}, bf16[2,2,2,128,128]{4,3,2,1,0:T(8,128)(2,1)S(1)}, u32[]{:S(2)}, u32[]{:S(2)}) collective-permute-start(bf16[2,2,2,128,128]{4,3,2,1,0:T(8,128)(2,1)S(1)} %copy_bitcast_fusion.near_ref), channel_id=1, source_target_pairs={{0,6},{6,0},{2,4},{4,2},{1,7},{7,1},{3,5},{5,3},{8,14},{14,8},{10,... | collective-permute-start | bytes 786440 | tf_op jit(solution)/shard_map/ppermute | solution.py:290

commit v5 on v4

--- a/solution.py
+++ b/solution.py
@@ -158,7 +158,7 @@
     col = lax.broadcasted_iota(jnp.int32, (1, 2 * count), 1)
     step = (col >= count).astype(jnp.int32)
     col = col - step * count
-    y = lax.axis_index("y") ^ step ^ (3 if far else 0)
+    y = lax.axis_index("y") ^ (3 * step) ^ (1 if far else 0)
     u = (col >> 4) * 64 + y * 16 + (col & 15)
     t = row + lax.broadcasted_iota(jnp.int32, (ROWS, 1), 0)
     return jnp.where(u <= jnp.minimum(t, length - 1), cont, NEG)
@@ -284,10 +284,10 @@
     own = lax.all_to_all(
         spread.reshape((16,) + pair.shape), ("x", "y"), 0, 0, tiled=True
     ).reshape(spread.shape)
-    beside = lax.ppermute(mine, "y", [(0, 1), (1, 0), (2, 3), (3, 2)])
+    beside = lax.ppermute(mine, "y", [(0, 3), (3, 0), (1, 2), (2, 1)])
     near = jnp.stack([mine, beside]).transpose(2, 3, 0, 1, 4, 5)
     near = near.reshape(2, 2, 2, 128, HEAD_SIZE)
-    far = lax.ppermute(near, "y", [(0, 3), (3, 0), (1, 2), (2, 1)])
+    far = lax.ppermute(near, "y", [(0, 1), (1, 0), (2, 3), (3, 2)])
     other = lax.ppermute(own, "c", [(0, 1), (1, 0)])
     wide = jax.ShapeDtypeStruct(queries.shape, jnp.float32)
     state = call(

time: 81.9 us -> 81.9 us (level)
  no operation moved by 1% of the time
where the time goes in v5:
time: 81.9 us; the launch traced here: 81.4 us
  starting transfers between devices  34.6 us (42%)
  waiting for transfers between devices  28.3 us (35%)
  Pallas kernels  9.82 us (12%)
  blocking collectives  8.52 us (10%)
    all_to_all x1, starting transfers between devices, local(): mine = lax.all_to_all(pieces, ('zl', 'c'), 0, 0, tiled=True)  13.7 us
    ppermute x1, starting transfers between devices, local(): pair = lax.ppermute(pair, AXES, block_moves())  10.3 us
    all_to_all x1, waiting for transfers between devices, local(): mine = lax.all_to_all(pieces, ('zl', 'c'), 0, 0, tiled=True)  9.97 us
    pallas_call x5, Pallas kernels, call(): pl.pallas_call(kernel, out_shape=out_shape, in_specs=[smem if operand.ndi...  9.82 us
    all_to_all x1, waiting for transfers between devices, local(): lax.all_to_all(spread.reshape((16,) + pair.shape), ('x', 'y'), 0, 0, tile...  9.5 us
    all_gather x1, blocking collectives, local(): pair = lax.all_gather(prompt, 'c')  8.52 us
    ppermute x1, waiting for transfers between devices, local(): beside = lax.ppermute(mine, 'y', [(0, 3), (3, 0), (1, 2), (2, 1)])  5.68 us
    all_to_all x1, starting transfers between devices, local(): lax.all_to_all(spread.reshape((16,) + pair.shape), ('x', 'y'), 0, 0, tile...  4.43 us
  transfers between devices with their start and end apart: 6, of which 5 were waited for; matrix products, arithmetic and copies ran while one was open for 0% of the time, Pallas kernels for 6%

profile of v5, /device:TPU:1, one launch (start us, length us, event | category | flops | bytes accessed | tf_op | source)
XLA Modules:
  0.0 81.4 jit_solution(9436381137040083928)
XLA Ops:
  0.0 8.5 %all-gather = bf16[4,32,128]{2,1,0:T(8,128)(2,1)S(1)} all-gather(bf16[2,32,128]{2,1,0:T(8,128)(2,1)} %param.7), channel_id=2, replica_groups=mesh['x'=4,'zh'=2,'zl'=8,'y'=4,'c'=2] {'c'}, dimensions={0}, use_global_device_ids=true | all-gather | bytes 49152 | tf_op jit(solution)/shard_map/all_gather | solution.py:279
  8.5 10.3 %collective-permute-start = (bf16[2,2,32,128]{3,2,1,0:T(8,128)(2,1)S(1)}, bf16[2,2,32,128]{3,2,1,0:T(8,128)(2,1)S(1)}, u32[]{:S(2)}, u32[]{:S(2)}) collective-permute-start(bf16[2,2,32,128]{3,2,1,0:T(8,128)(2,1)S(1)} %bitcast.19), channel_id=1, source_target_pairs={{56,0},{58,2},{60,4},{62,6},{48,1},{50,3},{52,5},{54,7},{40,128},{... | collective-permute-start | bytes 98312 | tf_op jit(solution)/shard_map/ppermute | solution.py:280
  18.8 1.0 %collective-permute-done.pair_ref = bf16[2,2,32,128]{3,2,1,0:T(8,128)(2,1)S(1)} collective-permute-done((bf16[2,2,32,128]{3,2,1,0:T(8,128)(2,1)S(1)}, bf16[2,2,32,128]{3,2,1,0:T(8,128)(2,1)S(1)}, u32[]{:S(2)}, u32[]{:S(2)}) %collective-permute-start) | collective-permute-done | bytes 32800 | tf_op jit(solution)/shard_map/ppermute | solution.py:280
  19.9 0.9 %shard_map.64 = bf16[4,4,2,2,32,128]{5,4,3,2,1,0:T(8,128)(2,1)} custom-call(bf16[2,2,32,128]{3,2,1,0:T(8,128)(2,1)S(1)} %collective-permute-done.pair_ref), custom_call_target="tpu_custom_call" | custom-call | bytes 2000000 | tf_op jit(solution)/shard_map/pallas_call | solution.py:261
  20.7 0.0 copy-start.2
  20.7 4.4 %all-to-all-start = ((bf16[16,2,2,32,128]{4,3,2,1,0:T(8,128)(2,1)}), bf16[16,2,2,32,128]{4,3,2,1,0:T(8,128)(2,1)S(1)}, u32[]{:S(2)}, u32[]{:S(2)}) async-start(bf16[16,2,2,32,128]{4,3,2,1,0:T(8,128)(2,1)} %bitcast.1), calls=%async_computation | async-start | bytes 1048576 | tf_op jit(solution)/shard_map/all_to_all | solution.py:284
  25.2 0.0 copy-done.2
  25.2 0.7 shard_map.65
  25.9 9.5 %all-to-all-done = bf16[16,2,2,32,128]{4,3,2,1,0:T(8,128)(2,1)S(1)} async-done(((bf16[16,2,2,32,128]{4,3,2,1,0:T(8,128)(2,1)}), bf16[16,2,2,32,128]{4,3,2,1,0:T(8,128)(2,1)S(1)}, u32[]{:S(2)}, u32[]{:S(2)}) %all-to-all-start) | async-done | bytes 524320 | tf_op jit(solution)/shard_map/all_to_all | solution.py:284
  35.4 13.7 %all-to-all-start.1 = ((bf16[16,2,2,8,128]{4,3,2,1,0:T(8,128)(2,1)}), bf16[16,2,2,8,128]{4,3,2,1,0:T(8,128)(2,1)S(1)}, u32[]{:S(2)}, u32[]{:S(2)}) async-start(bf16[16,2,2,8,128]{4,3,2,1,0:T(8,128)(2,1)} %bitcast.3), calls=%async_computation.1 | async-start | bytes 262144 | tf_op jit(solution)/shard_map/all_to_all | solution.py:278
  49.0 2.0 %collective-permute-start.1 = (bf16[4,4,2,2,32,128]{5,4,3,2,1,0:T(8,128)(2,1)S(1)}, bf16[4,4,2,2,32,128]{5,4,3,2,1,0:T(8,128)(2,1)S(1)}, u32[]{:S(2)}, u32[]{:S(2)}) collective-permute-start(bf16[4,4,2,2,32,128]{5,4,3,2,1,0:T(8,128)(2,1)S(1)} %bitcast.12), channel_id=1, source_target_pairs={{0,1},{1,0},{2,3},{3,2},{4,5},{5,4},{6,7},{7,6},{8,9},{9,8},{10,11... | collective-permute-start | bytes 1572872 | tf_op jit(solution)/shard_map/ppermute | solution.py:291
  51.0 10.0 %all-to-all-done.1 = bf16[16,2,2,8,128]{4,3,2,1,0:T(8,128)(2,1)S(1)} async-done(((bf16[16,2,2,8,128]{4,3,2,1,0:T(8,128)(2,1)}), bf16[16,2,2,8,128]{4,3,2,1,0:T(8,128)(2,1)S(1)}, u32[]{:S(2)}, u32[]{:S(2)}) %all-to-all-start.1) | async-done | bytes 131104 | tf_op jit(solution)/shard_map/all_to_all | solution.py:278
  61.0 2.2 %collective-permute-start.2 = (bf16[16,2,2,8,128]{4,3,2,1,0:T(8,128)(2,1)S(1)}, bf16[16,2,2,8,128]{4,3,2,1,0:T(8,128)(2,1)S(1)}, u32[]{:S(2)}, u32[]{:S(2)}) collective-permute-start(bf16[16,2,2,8,128]{4,3,2,1,0:T(8,128)(2,1)S(1)} %all-to-all-done.1), channel_id=1, source_target_pairs={{0,6},{6,0},{2,4},{4,2},{1,7},{7,1},{3,5},{5,3},{8,14},{14,8},{10,... | collective-permute-start | bytes 393224 | tf_op jit(solution)/shard_map/ppermute | solution.py:287
  63.2 5.7 %collective-permute-done.2 = bf16[16,2,2,8,128]{4,3,2,1,0:T(8,128)(2,1)S(1)} collective-permute-done((bf16[16,2,2,8,128]{4,3,2,1,0:T(8,128)(2,1)S(1)}, bf16[16,2,2,8,128]{4,3,2,1,0:T(8,128)(2,1)S(1)}, u32[]{:S(2)}, u32[]{:S(2)}) %collective-permute-start.2) | collective-permute-done | bytes 131104 | tf_op jit(solution)/shard_map/ppermute | solution.py:287
  68.9 0.0 copy-start
  68.9 0.0 copy-start.1
  68.9 0.0 copy-start.3
  69.0 0.0 copy-start.4
  69.0 2.1 %collective-permute-start.3 = (bf16[2,2,2,128,128]{4,3,2,1,0:T(8,128)(2,1)S(1)}, bf16[2,2,2,128,128]{4,3,2,1,0:T(8,128)(2,1)S(1)}, u32[]{:S(2)}, u32[]{:S(2)}) collective-permute-start(bf16[2,2,2,128,128]{4,3,2,1,0:T(8,128)(2,1)S(1)} %copy_bitcast_fusion.near_ref), channel_id=1, source_target_pairs={{0,2},{2,0},{4,6},{6,4},{1,3},{3,1},{5,7},{7,5},{8,10},{10,8},{12,... | collective-permute-start | bytes 786440 | tf_op jit(solution)/shard_map/ppermute | solution.py:290
  71.0 0.0 copy-done
  71.0 0.0 copy-done.1
  71.0 0.0 copy-done.3
  71.1 0.0 copy-done.4
  71.1 1.8 %shard_map.66 = (f32[2,512,128]{2,1,0:T(8,128)S(1)}, f32[2,512,128]{2,1,0:T(8,128)S(1)}, f32[2,512,128]{2,1,0:T(8,128)S(1)}) custom-call(bf16[2,512,128]{2,1,0:T(8,128)(2,1)S(1)} %copy-done, bf16[2,2,2,128,128]{4,3,2,1,0:T(8,128)(2,1)S(1)} %copy_bitcast_fusion.near_ref, s32[16]{0:T(128)S(1)} %copy-done.3, s32[16]{0:T(128)S(1)} %copy-done.4, ...), custom_call_target="tpu_custom_call" | custom-call | flops 100000000 | bytes 2000000 | tf_op jit(solution)/shard_map/pallas_call | solution.py:261
  72.8 2.8 %shard_map.67 = (f32[2,512,128]{2,1,0:T(8,128)S(1)}, f32[2,512,128]{2,1,0:T(8,128)S(1)}, f32[2,512,128]{2,1,0:T(8,128)S(1)}) custom-call(bf16[2,512,128]{2,1,0:T(8,128)(2,1)S(1)} %copy-done, bf16[4,4,2,2,32,128]{5,4,3,2,1,0:T(8,128)(2,1)S(1)} %bitcast.13, s32[8,2,128]{2,1,0:T(2,128)S(1)} %bitcast.15, s32[16]{0:T(128)S(1)} %copy-done.3, s32[16]{0:T(128)S(1)} %copy-done.4, ...), custom_call_target="tpu_custom_call" | custom-call | flops 550000000 | bytes 2000000 | tf_op jit(solution)/shard_map/pallas_call | solution.py:261
  75.6 2.1 %collective-permute-done.3.far_ref = bf16[2,2,2,128,128]{4,3,2,1,0:T(8,128)(2,1)S(1)} collective-permute-done((bf16[2,2,2,128,128]{4,3,2,1,0:T(8,128)(2,1)S(1)}, bf16[2,2,2,128,128]{4,3,2,1,0:T(8,128)(2,1)S(1)}, u32[]{:S(2)}, u32[]{:S(2)}) %collective-permute-start.3) | collective-permute-done | bytes 262176 | tf_op jit(solution)/shard_map/ppermute | solution.py:290
  77.7 0.0 collective-permute-done.1.half_ref
  77.7 3.7 %shard_map.68 = bf16[2,512,128]{2,1,0:T(8,128)(2,1)} custom-call(bf16[2,512,128]{2,1,0:T(8,128)(2,1)S(1)} %copy-done, bf16[4,4,2,2,32,128]{5,4,3,2,1,0:T(8,128)(2,1)S(1)} %collective-permute-done.1.half_ref, bf16[2,2,2,128,128]{4,3,2,1,0:T(8,128)(2,1)S(1)} %collective-permute-done.3.far_ref, s32[8,2,128]{2,1,0:T(2,128)S(1)} %bitcast.16, s32[16]{0:T(128)S(1)} %copy-done.3, ...), custom_call_target="tpu_custom_call" | custom-call | flops 650000000 | bytes 2000000 | tf_op jit(solution)/shard_map/pallas_call | solution.py:261
  (1 shorter events, 0.0 us)
Async XLA Ops:
  8.5 11.3 %collective-permute-start = (bf16[2,2,32,128]{3,2,1,0:T(8,128)(2,1)S(1)}, bf16[2,2,32,128]{3,2,1,0:T(8,128)(2,1)S(1)}, u32[]{:S(2)}, u32[]{:S(2)}) collective-permute-start(bf16[2,2,32,128]{3,2,1,0:T(8,128)(2,1)S(1)} %bitcast.19), channel_id=1, source_target_pairs={{56,0},{58,2},{60,4},{62,6},{48,1},{50,3},{52,5},{54,7},{40,128},{... | collective-permute-start | bytes 98312 | tf_op jit(solution)/shard_map/ppermute | solution.py:280
  20.7 4.4 %copy-start.2 = (bf16[2,2,8,1024]{3,2,1,0:T(8,128)(2,1)S(1)}, bf16[2,2,8,1024]{3,2,1,0:T(8,128)(2,1)}, u32[]{:S(2)}) copy-start(bf16[2,2,8,1024]{3,2,1,0:T(8,128)(2,1)} %cont_ref.1) | copy-start | bytes 196612
  20.7 14.6 %all-to-all-start = ((bf16[16,2,2,32,128]{4,3,2,1,0:T(8,128)(2,1)}), bf16[16,2,2,32,128]{4,3,2,1,0:T(8,128)(2,1)S(1)}, u32[]{:S(2)}, u32[]{:S(2)}) async-start(bf16[16,2,2,32,128]{4,3,2,1,0:T(8,128)(2,1)} %bitcast.1), calls=%async_computation | async-start | bytes 1048576 | tf_op jit(solution)/shard_map/all_to_all | solution.py:284
  35.4 25.7 %all-to-all-start.1 = ((bf16[16,2,2,8,128]{4,3,2,1,0:T(8,128)(2,1)}), bf16[16,2,2,8,128]{4,3,2,1,0:T(8,128)(2,1)S(1)}, u32[]{:S(2)}, u32[]{:S(2)}) async-start(bf16[16,2,2,8,128]{4,3,2,1,0:T(8,128)(2,1)} %bitcast.3), calls=%async_computation.1 | async-start | bytes 262144 | tf_op jit(solution)/shard_map/all_to_all | solution.py:278
  49.0 28.7 %collective-permute-start.1 = (bf16[4,4,2,2,32,128]{5,4,3,2,1,0:T(8,128)(2,1)S(1)}, bf16[4,4,2,2,32,128]{5,4,3,2,1,0:T(8,128)(2,1)S(1)}, u32[]{:S(2)}, u32[]{:S(2)}) collective-permute-start(bf16[4,4,2,2,32,128]{5,4,3,2,1,0:T(8,128)(2,1)S(1)} %bitcast.12), channel_id=1, source_target_pairs={{0,1},{1,0},{2,3},{3,2},{4,5},{5,4},{6,7},{7,6},{8,9},{9,8},{10,11... | collective-permute-start | bytes 1572872 | tf_op jit(solution)/shard_map/ppermute | solution.py:291
  61.0 7.9 %collective-permute-start.2 = (bf16[16,2,2,8,128]{4,3,2,1,0:T(8,128)(2,1)S(1)}, bf16[16,2,2,8,128]{4,3,2,1,0:T(8,128)(2,1)S(1)}, u32[]{:S(2)}, u32[]{:S(2)}) collective-permute-start(bf16[16,2,2,8,128]{4,3,2,1,0:T(8,128)(2,1)S(1)} %all-to-all-done.1), channel_id=1, source_target_pairs={{0,6},{6,0},{2,4},{4,2},{1,7},{7,1},{3,5},{5,3},{8,14},{14,8},{10,... | collective-permute-start | bytes 393224 | tf_op jit(solution)/shard_map/ppermute | solution.py:287
  68.9 2.1 %copy-start = (bf16[2,512,128]{2,1,0:T(8,128)(2,1)S(1)}, bf16[2,512,128]{2,1,0:T(8,128)(2,1)}, u32[]{:S(2)}) copy-start(bf16[2,512,128]{2,1,0:T(8,128)(2,1)} %q_ref.5) | copy-start | bytes 786436
  68.9 2.1 %copy-start.1 = (s32[2048]{0:T(1024)S(1)}, s32[2048]{0:T(1024)}, u32[]{:S(2)}) copy-start(s32[2048]{0:T(1024)} %param.9) | copy-start | bytes 24580
  68.9 2.1 %copy-start.3 = (s32[16]{0:T(128)S(1)}, s32[16]{0:T(128)}, u32[]{:S(2)}) copy-start(s32[16]{0:T(128)} %lengths_ref.5) | copy-start | bytes 196
  69.0 2.1 %copy-start.4 = (s32[16]{0:T(128)S(1)}, s32[16]{0:T(128)}, u32[]{:S(2)}) copy-start(s32[16]{0:T(128)} %offsets_ref.5) | copy-start | bytes 196
  69.0 8.8 %collective-permute-start.3 = (bf16[2,2,2,128,128]{4,3,2,1,0:T(8,128)(2,1)S(1)}, bf16[2,2,2,128,128]{4,3,2,1,0:T(8,128)(2,1)S(1)}, u32[]{:S(2)}, u32[]{:S(2)}) collective-permute-start(bf16[2,2,2,128,128]{4,3,2,1,0:T(8,128)(2,1)S(1)} %copy_bitcast_fusion.near_ref), channel_id=1, source_target_pairs={{0,2},{2,0},{4,6},{6,4},{1,3},{3,1},{5,7},{7,5},{8,10},{10,8},{12,... | collective-permute-start | bytes 786440 | tf_op jit(solution)/shard_map/ppermute | solution.py:290

commit v6 on v5

--- a/solution.py
+++ b/solution.py
@@ -93,9 +93,12 @@
         consume(*tile, part)
 
 
-def live_rows(lengths_ref, product, consume, blank=None):
+def live_rows(lengths_ref, product, consume, blank=None, ready=None):
     base = first_sample()
     run_tiles([(here, row) for here in range(2) for row in (0, ROWS)], product, consume)
+    if ready is not None:
+        for here in range(2):
+            ready(here, 0)
     for here in range(2):
         length = lengths_ref[base + here]
         tiles = [(here, 2 * ROWS), (here, 3 * ROWS)]
@@ -116,6 +119,9 @@
             def _():
                 for tile in tiles:
                     blank(*tile)
+
+        if ready is not None:
+            ready(here, 2 * ROWS)
 
 
 def prompt_side(half_ref, kind):
@@ -226,6 +232,8 @@
     total_ref,
     mixed_ref,
     out_ref,
+    held,
+    sent,
 ):
     base = first_sample()
     biases = prompt_biases(1 - lax.axis_index("c"), owner_ref, offsets_ref)
@@ -247,22 +255,36 @@
         mixed += more[0] + mixed_ref[here, rows] * shrink
         total += more[1] + total_ref[here, rows] * shrink
         t = row + lax.broadcasted_iota(jnp.int32, (ROWS, 1), 0)
-        out_ref[here, rows] = jnp.where(t < length, mixed / total, 0.0).astype(jnp.bfloat16)
+        held[here, rows] = jnp.where(t < length, mixed / total, 0.0).astype(jnp.bfloat16)
 
     def blank(here, row):
-        out_ref[here, row : row + ROWS] = jnp.zeros((ROWS, HEAD_SIZE), jnp.bfloat16)
-
-    live_rows(lengths_ref, product, consume, blank)
-
-
-def call(kernel, out_shape, flops, *operands):
+        held[here, row : row + ROWS] = jnp.zeros((ROWS, HEAD_SIZE), jnp.bfloat16)
+
+    copies = []
+
+    def ready(here, row):
+        rows = pl.ds(row, 2 * ROWS)
+        copies.append(
+            pltpu.make_async_copy(
+                held.at[here, rows], out_ref.at[here, rows], sent.at[here, row // (2 * ROWS)]
+            )
+        )
+        copies[-1].start()
+
+    live_rows(lengths_ref, product, consume, blank, ready)
+    for copy in copies:
+        copy.wait()
+
+
+def call(kernel, out_shape, flops, *operands, out_space=pltpu.VMEM, scratch=()):
     vmem = pl.BlockSpec(memory_space=pltpu.VMEM)
     smem = pl.BlockSpec(memory_space=pltpu.SMEM)
     return pl.pallas_call(
         kernel,
         out_shape=out_shape,
         in_specs=[smem if operand.ndim == 1 else vmem for operand in operands],
-        out_specs=jax.tree.map(lambda _: vmem, out_shape),
+        out_specs=jax.tree.map(lambda _: pl.BlockSpec(memory_space=out_space), out_shape),
+        scratch_shapes=scratch,
         compiler_params=pltpu.CompilerParams(vmem_limit_bytes=24 << 20),
         cost_estimate=pl.CostEstimate(
             flops=flops, transcendentals=flops // 512, bytes_accessed=2000000
@@ -278,9 +300,7 @@
     mine = lax.all_to_all(pieces, ("zl", "c"), 0, 0, tiled=True)
     pair = lax.all_gather(prompt, "c")
     pair = lax.ppermute(pair, AXES, block_moves())
-    spread = call(
-        repeat_blocks, jax.ShapeDtypeStruct((4, 4) + pair.shape, pair.dtype), 0, pair
-    )
+    spread = call(repeat_blocks, jax.ShapeDtypeStruct((4, 4) + pair.shape, pair.dtype), 0, pair)
     own = lax.all_to_all(
         spread.reshape((16,) + pair.shape), ("x", "y"), 0, 0, tiled=True
     ).reshape(spread.shape)
@@ -322,6 +342,11 @@
         cont_lengths,
         branch_offsets,
         *state,
+        out_space=pltpu.HBM,
+        scratch=[
+            pltpu.VMEM(queries.shape, jnp.bfloat16),
+            pltpu.SemaphoreType.DMA((2, 2)),
+        ],
     )
 
 

time: 81.9 us -> 81.8 us (level)
  no operation moved by 1% of the time
where the time goes in v6:
time: 81.8 us; the launch traced here: 81.4 us
  starting transfers between devices  34.6 us (42%)
  waiting for transfers between devices  28.3 us (35%)
  Pallas kernels  9.78 us (12%)
  blocking collectives  8.52 us (10%)
    all_to_all x1, starting transfers between devices, local(): mine = lax.all_to_all(pieces, ('zl', 'c'), 0, 0, tiled=True)  13.7 us
    ppermute x1, starting transfers between devices, local(): pair = lax.ppermute(pair, AXES, block_moves())  10.3 us
    all_to_all x1, waiting for transfers between devices, local(): mine = lax.all_to_all(pieces, ('zl', 'c'), 0, 0, tiled=True)  9.97 us
    pallas_call x5, Pallas kernels, call(): pl.pallas_call(kernel, out_shape=out_shape, in_specs=[smem if operand.ndi...  9.78 us
    all_to_all x1, waiting for transfers between devices, local(): lax.all_to_all(spread.reshape((16,) + pair.shape), ('x', 'y'), 0, 0, tile...  9.5 us
    all_gather x1, blocking collectives, local(): pair = lax.all_gather(prompt, 'c')  8.52 us
    ppermute x1, waiting for transfers between devices, local(): beside = lax.ppermute(mine, 'y', [(0, 3), (3, 0), (1, 2), (2, 1)])  5.68 us
    all_to_all x1, starting transfers between devices, local(): lax.all_to_all(spread.reshape((16,) + pair.shape), ('x', 'y'), 0, 0, tile...  4.43 us
  transfers between devices with their start and end apart: 6, of which 5 were waited for; matrix products, arithmetic and copies ran while one was open for 0% of the time, Pallas kernels for 6%

profile of v6, /device:TPU:1, one launch (start us, length us, event | category | flops | bytes accessed | tf_op | source)
XLA Modules:
  0.0 81.4 jit_solution(8305728005605753382)
XLA Ops:
  0.0 8.5 %all-gather = bf16[4,32,128]{2,1,0:T(8,128)(2,1)S(1)} all-gather(bf16[2,32,128]{2,1,0:T(8,128)(2,1)} %param.7), channel_id=2, replica_groups=mesh['x'=4,'zh'=2,'zl'=8,'y'=4,'c'=2] {'c'}, dimensions={0}, use_global_device_ids=true | all-gather | bytes 49152 | tf_op jit(solution)/shard_map/all_gather | solution.py:301
  8.5 10.3 %collective-permute-start = (bf16[2,2,32,128]{3,2,1,0:T(8,128)(2,1)S(1)}, bf16[2,2,32,128]{3,2,1,0:T(8,128)(2,1)S(1)}, u32[]{:S(2)}, u32[]{:S(2)}) collective-permute-start(bf16[2,2,32,128]{3,2,1,0:T(8,128)(2,1)S(1)} %bitcast.19), channel_id=1, source_target_pairs={{56,0},{58,2},{60,4},{62,6},{48,1},{50,3},{52,5},{54,7},{40,128},{... | collective-permute-start | bytes 98312 | tf_op jit(solution)/shard_map/ppermute | solution.py:302
  18.8 1.0 %collective-permute-done.pair_ref = bf16[2,2,32,128]{3,2,1,0:T(8,128)(2,1)S(1)} collective-permute-done((bf16[2,2,32,128]{3,2,1,0:T(8,128)(2,1)S(1)}, bf16[2,2,32,128]{3,2,1,0:T(8,128)(2,1)S(1)}, u32[]{:S(2)}, u32[]{:S(2)}) %collective-permute-start) | collective-permute-done | bytes 32800 | tf_op jit(solution)/shard_map/ppermute | solution.py:302
  19.9 0.9 %shard_map.64 = bf16[4,4,2,2,32,128]{5,4,3,2,1,0:T(8,128)(2,1)} custom-call(bf16[2,2,32,128]{3,2,1,0:T(8,128)(2,1)S(1)} %collective-permute-done.pair_ref), custom_call_target="tpu_custom_call" | custom-call | bytes 2000000 | tf_op jit(solution)/shard_map/pallas_call | solution.py:282
  20.7 0.0 copy-start.2
  20.7 4.4 %all-to-all-start = ((bf16[16,2,2,32,128]{4,3,2,1,0:T(8,128)(2,1)}), bf16[16,2,2,32,128]{4,3,2,1,0:T(8,128)(2,1)S(1)}, u32[]{:S(2)}, u32[]{:S(2)}) async-start(bf16[16,2,2,32,128]{4,3,2,1,0:T(8,128)(2,1)} %bitcast.1), calls=%async_computation | async-start | bytes 1048576 | tf_op jit(solution)/shard_map/all_to_all | solution.py:304
  25.2 0.0 copy-done.2
  25.2 0.7 shard_map.65
  25.9 9.5 %all-to-all-done = bf16[16,2,2,32,128]{4,3,2,1,0:T(8,128)(2,1)S(1)} async-done(((bf16[16,2,2,32,128]{4,3,2,1,0:T(8,128)(2,1)}), bf16[16,2,2,32,128]{4,3,2,1,0:T(8,128)(2,1)S(1)}, u32[]{:S(2)}, u32[]{:S(2)}) %all-to-all-start) | async-done | bytes 524320 | tf_op jit(solution)/shard_map/all_to_all | solution.py:304
  35.4 13.7 %all-to-all-start.1 = ((bf16[16,2,2,8,128]{4,3,2,1,0:T(8,128)(2,1)}), bf16[16,2,2,8,128]{4,3,2,1,0:T(8,128)(2,1)S(1)}, u32[]{:S(2)}, u32[]{:S(2)}) async-start(bf16[16,2,2,8,128]{4,3,2,1,0:T(8,128)(2,1)} %bitcast.3), calls=%async_computation.1 | async-start | bytes 262144 | tf_op jit(solution)/shard_map/all_to_all | solution.py:300
  49.0 2.0 %collective-permute-start.1 = (bf16[4,4,2,2,32,128]{5,4,3,2,1,0:T(8,128)(2,1)S(1)}, bf16[4,4,2,2,32,128]{5,4,3,2,1,0:T(8,128)(2,1)S(1)}, u32[]{:S(2)}, u32[]{:S(2)}) collective-permute-start(bf16[4,4,2,2,32,128]{5,4,3,2,1,0:T(8,128)(2,1)S(1)} %bitcast.12), channel_id=1, source_target_pairs={{0,1},{1,0},{2,3},{3,2},{4,5},{5,4},{6,7},{7,6},{8,9},{9,8},{10,11... | collective-permute-start | bytes 1572872 | tf_op jit(solution)/shard_map/ppermute | solution.py:311
  51.0 10.0 %all-to-all-done.1 = bf16[16,2,2,8,128]{4,3,2,1,0:T(8,128)(2,1)S(1)} async-done(((bf16[16,2,2,8,128]{4,3,2,1,0:T(8,128)(2,1)}), bf16[16,2,2,8,128]{4,3,2,1,0:T(8,128)(2,1)S(1)}, u32[]{:S(2)}, u32[]{:S(2)}) %all-to-all-start.1) | async-done | bytes 131104 | tf_op jit(solution)/shard_map/all_to_all | solution.py:300
  61.0 2.2 %collective-permute-start.2 = (bf16[16,2,2,8,128]{4,3,2,1,0:T(8,128)(2,1)S(1)}, bf16[16,2,2,8,128]{4,3,2,1,0:T(8,128)(2,1)S(1)}, u32[]{:S(2)}, u32[]{:S(2)}) collective-permute-start(bf16[16,2,2,8,128]{4,3,2,1,0:T(8,128)(2,1)S(1)} %all-to-all-done.1), channel_id=1, source_target_pairs={{0,6},{6,0},{2,4},{4,2},{1,7},{7,1},{3,5},{5,3},{8,14},{14,8},{10,... | collective-permute-start | bytes 393224 | tf_op jit(solution)/shard_map/ppermute | solution.py:307
  63.2 5.7 %collective-permute-done.2 = bf16[16,2,2,8,128]{4,3,2,1,0:T(8,128)(2,1)S(1)} collective-permute-done((bf16[16,2,2,8,128]{4,3,2,1,0:T(8,128)(2,1)S(1)}, bf16[16,2,2,8,128]{4,3,2,1,0:T(8,128)(2,1)S(1)}, u32[]{:S(2)}, u32[]{:S(2)}) %collective-permute-start.2) | collective-permute-done | bytes 131104 | tf_op jit(solution)/shard_map/ppermute | solution.py:307
  68.9 0.0 copy-start
  68.9 0.0 copy-start.1
  68.9 0.0 copy-start.3
  69.0 0.0 copy-start.4
  69.0 2.1 %collective-permute-start.3 = (bf16[2,2,2,128,128]{4,3,2,1,0:T(8,128)(2,1)S(1)}, bf16[2,2,2,128,128]{4,3,2,1,0:T(8,128)(2,1)S(1)}, u32[]{:S(2)}, u32[]{:S(2)}) collective-permute-start(bf16[2,2,2,128,128]{4,3,2,1,0:T(8,128)(2,1)S(1)} %copy_bitcast_fusion.near_ref), channel_id=1, source_target_pairs={{0,2},{2,0},{4,6},{6,4},{1,3},{3,1},{5,7},{7,5},{8,10},{10,8},{12,... | collective-permute-start | bytes 786440 | tf_op jit(solution)/shard_map/ppermute | solution.py:310
  71.0 0.0 copy-done
  71.0 0.0 copy-done.1
  71.0 0.0 copy-done.3
  71.1 0.0 copy-done.4
  71.1 1.8 %shard_map.66 = (f32[2,512,128]{2,1,0:T(8,128)S(1)}, f32[2,512,128]{2,1,0:T(8,128)S(1)}, f32[2,512,128]{2,1,0:T(8,128)S(1)}) custom-call(bf16[2,512,128]{2,1,0:T(8,128)(2,1)S(1)} %copy-done, bf16[2,2,2,128,128]{4,3,2,1,0:T(8,128)(2,1)S(1)} %copy_bitcast_fusion.near_ref, s32[16]{0:T(128)S(1)} %copy-done.3, s32[16]{0:T(128)S(1)} %copy-done.4, ...), custom_call_target="tpu_custom_call" | custom-call | flops 100000000 | bytes 2000000 | tf_op jit(solution)/shard_map/pallas_call | solution.py:282
  72.8 2.8 %shard_map.67 = (f32[2,512,128]{2,1,0:T(8,128)S(1)}, f32[2,512,128]{2,1,0:T(8,128)S(1)}, f32[2,512,128]{2,1,0:T(8,128)S(1)}) custom-call(bf16[2,512,128]{2,1,0:T(8,128)(2,1)S(1)} %copy-done, bf16[4,4,2,2,32,128]{5,4,3,2,1,0:T(8,128)(2,1)S(1)} %bitcast.13, s32[8,2,128]{2,1,0:T(2,128)S(1)} %bitcast.15, s32[16]{0:T(128)S(1)} %copy-done.3, s32[16]{0:T(128)S(1)} %copy-done.4, ...), custom_call_target="tpu_custom_call" | custom-call | flops 550000000 | bytes 2000000 | tf_op jit(solution)/shard_map/pallas_call | solution.py:282
  75.6 2.1 %collective-permute-done.3.far_ref = bf16[2,2,2,128,128]{4,3,2,1,0:T(8,128)(2,1)S(1)} collective-permute-done((bf16[2,2,2,128,128]{4,3,2,1,0:T(8,128)(2,1)S(1)}, bf16[2,2,2,128,128]{4,3,2,1,0:T(8,128)(2,1)S(1)}, u32[]{:S(2)}, u32[]{:S(2)}) %collective-permute-start.3) | collective-permute-done | bytes 262176 | tf_op jit(solution)/shard_map/ppermute | solution.py:310
  77.7 0.0 collective-permute-done.1.half_ref
  77.7 3.7 %shard_map.68 = bf16[2,512,128]{2,1,0:T(8,128)(2,1)} custom-call(bf16[2,512,128]{2,1,0:T(8,128)(2,1)S(1)} %copy-done, bf16[4,4,2,2,32,128]{5,4,3,2,1,0:T(8,128)(2,1)S(1)} %collective-permute-done.1.half_ref, bf16[2,2,2,128,128]{4,3,2,1,0:T(8,128)(2,1)S(1)} %collective-permute-done.3.far_ref, s32[8,2,128]{2,1,0:T(2,128)S(1)} %bitcast.16, s32[16]{0:T(128)S(1)} %copy-done.3, ...), custom_call_target="tpu_custom_call" | custom-call | flops 650000000 | bytes 2000000 | tf_op jit(solution)/shard_map/pallas_call | solution.py:282
  (1 shorter events, 0.0 us)
Async XLA Ops:
  8.5 11.3 %collective-permute-start = (bf16[2,2,32,128]{3,2,1,0:T(8,128)(2,1)S(1)}, bf16[2,2,32,128]{3,2,1,0:T(8,128)(2,1)S(1)}, u32[]{:S(2)}, u32[]{:S(2)}) collective-permute-start(bf16[2,2,32,128]{3,2,1,0:T(8,128)(2,1)S(1)} %bitcast.19), channel_id=1, source_target_pairs={{56,0},{58,2},{60,4},{62,6},{48,1},{50,3},{52,5},{54,7},{40,128},{... | collective-permute-start | bytes 98312 | tf_op jit(solution)/shard_map/ppermute | solution.py:302
  20.7 4.4 %copy-start.2 = (bf16[2,2,8,1024]{3,2,1,0:T(8,128)(2,1)S(1)}, bf16[2,2,8,1024]{3,2,1,0:T(8,128)(2,1)}, u32[]{:S(2)}) copy-start(bf16[2,2,8,1024]{3,2,1,0:T(8,128)(2,1)} %cont_ref.1) | copy-start | bytes 196612
  20.7 14.6 %all-to-all-start = ((bf16[16,2,2,32,128]{4,3,2,1,0:T(8,128)(2,1)}), bf16[16,2,2,32,128]{4,3,2,1,0:T(8,128)(2,1)S(1)}, u32[]{:S(2)}, u32[]{:S(2)}) async-start(bf16[16,2,2,32,128]{4,3,2,1,0:T(8,128)(2,1)} %bitcast.1), calls=%async_computation | async-start | bytes 1048576 | tf_op jit(solution)/shard_map/all_to_all | solution.py:304
  35.4 25.7 %all-to-all-start.1 = ((bf16[16,2,2,8,128]{4,3,2,1,0:T(8,128)(2,1)}), bf16[16,2,2,8,128]{4,3,2,1,0:T(8,128)(2,1)S(1)}, u32[]{:S(2)}, u32[]{:S(2)}) async-start(bf16[16,2,2,8,128]{4,3,2,1,0:T(8,128)(2,1)} %bitcast.3), calls=%async_computation.1 | async-start | bytes 262144 | tf_op jit(solution)/shard_map/all_to_all | solution.py:300
  49.0 28.7 %collective-permute-start.1 = (bf16[4,4,2,2,32,128]{5,4,3,2,1,0:T(8,128)(2,1)S(1)}, bf16[4,4,2,2,32,128]{5,4,3,2,1,0:T(8,128)(2,1)S(1)}, u32[]{:S(2)}, u32[]{:S(2)}) collective-permute-start(bf16[4,4,2,2,32,128]{5,4,3,2,1,0:T(8,128)(2,1)S(1)} %bitcast.12), channel_id=1, source_target_pairs={{0,1},{1,0},{2,3},{3,2},{4,5},{5,4},{6,7},{7,6},{8,9},{9,8},{10,11... | collective-permute-start | bytes 1572872 | tf_op jit(solution)/shard_map/ppermute | solution.py:311
  61.0 7.9 %collective-permute-start.2 = (bf16[16,2,2,8,128]{4,3,2,1,0:T(8,128)(2,1)S(1)}, bf16[16,2,2,8,128]{4,3,2,1,0:T(8,128)(2,1)S(1)}, u32[]{:S(2)}, u32[]{:S(2)}) collective-permute-start(bf16[16,2,2,8,128]{4,3,2,1,0:T(8,128)(2,1)S(1)} %all-to-all-done.1), channel_id=1, source_target_pairs={{0,6},{6,0},{2,4},{4,2},{1,7},{7,1},{3,5},{5,3},{8,14},{14,8},{10,... | collective-permute-start | bytes 393224 | tf_op jit(solution)/shard_map/ppermute | solution.py:307
  68.9 2.1 %copy-start = (bf16[2,512,128]{2,1,0:T(8,128)(2,1)S(1)}, bf16[2,512,128]{2,1,0:T(8,128)(2,1)}, u32[]{:S(2)}) copy-start(bf16[2,512,128]{2,1,0:T(8,128)(2,1)} %q_ref.5) | copy-start | bytes 786436
  68.9 2.1 %copy-start.1 = (s32[2048]{0:T(1024)S(1)}, s32[2048]{0:T(1024)}, u32[]{:S(2)}) copy-start(s32[2048]{0:T(1024)} %param.9) | copy-start | bytes 24580
  68.9 2.1 %copy-start.3 = (s32[16]{0:T(128)S(1)}, s32[16]{0:T(128)}, u32[]{:S(2)}) copy-start(s32[16]{0:T(128)} %lengths_ref.5) | copy-start | bytes 196
  69.0 2.1 %copy-start.4 = (s32[16]{0:T(128)S(1)}, s32[16]{0:T(128)}, u32[]{:S(2)}) copy-start(s32[16]{0:T(128)} %offsets_ref.5) | copy-start | bytes 196
  69.0 8.8 %collective-permute-start.3 = (bf16[2,2,2,128,128]{4,3,2,1,0:T(8,128)(2,1)S(1)}, bf16[2,2,2,128,128]{4,3,2,1,0:T(8,128)(2,1)S(1)}, u32[]{:S(2)}, u32[]{:S(2)}) collective-permute-start(bf16[2,2,2,128,128]{4,3,2,1,0:T(8,128)(2,1)S(1)} %copy_bitcast_fusion.near_ref), channel_id=1, source_target_pairs={{0,2},{2,0},{4,6},{6,4},{1,3},{3,1},{5,7},{7,5},{8,10},{10,8},{12,... | collective-permute-start | bytes 786440 | tf_op jit(solution)/shard_map/ppermute | solution.py:310
